TPU v7x, 128 devices: a whole 4x4x4 slice. The times are simulated.
128 devices in a mesh: dp: 32 (over z, x, core), rep: 4 (over y).
Axes of the slice: x: 4, y: 4, z: 4, core: 2. Of those that a mesh axis runs over, the one named last changes fastest.
Arguments:
- token_inputs: bfloat16 [65536, 2048], P(('dp', 'rep')), may hold values from -12 to 12
- cotangent: bfloat16 [65536, 2048], P(('dp', 'rep')), may hold values from -24 to 24
- gate_preact: bfloat16 [65536, 768], P(('dp', 'rep')), may hold values from -6 to 6
- up_preact: bfloat16 [65536, 768], P(('dp', 'rep')), may hold values from -6 to 6
- down_weight: bfloat16 [2, 768, 2048], P(None, None, 'dp'), may hold values from -0.21875 to 0.21875
- block_expert: int32 [512], P(('dp', 'rep')), may hold values from 0 to 1
- block_count: int32 [512], P(('dp', 'rep')), may hold values from 1 to 128, as said below
Outputs:
- update: bfloat16 [2, 3, 768, 2048], P(None, None, None, 'dp')
Inputs may be any that keep to these rules, and one draw needn't show every extreme that they name: `block_count`: live rows of a block, at most 128; in every draw some block is full.
All inputs are finite; a program needn't handle non-finite values.
Results may differ from a plain program's by a relative error of at most 0.02.
Values may be sent and summed in bfloat16 or wider, within the bound.
A program may use at most 128 MiB of HBM per device.

v0:
```python
import math

import jax
import jax.numpy as jnp
from jax import lax
from jax.sharding import Mesh
from jax.sharding import PartitionSpec as P

D = 2048
ITERS = 2
DP = ("dp_0", "dp_1", "dp_2")
DP_REP = ("dp_0", "dp_1", "dp_2", "rep")


ns_first = 3.4445
ns_second = -4.775
ns_third = 2.0315
norm_eps = 1e-07


def cut_along(value, dim, count):
    shape = value.shape
    blocks = value.reshape(*shape[:dim], count, shape[dim] // count, *shape[dim + 1 :])
    return jnp.moveaxis(blocks, dim, 0)


def sum_by_chip(value, chips, core, dim):
    sizes = (lax.axis_size(chips), lax.axis_size(core))
    blocks = cut_along(value, dim, sizes[0] * sizes[1])
    inside = blocks.shape[1:]
    blocks = blocks.reshape(*sizes, *inside).swapaxes(0, 1).reshape(-1, *inside)
    blocks = lax.psum_scatter(blocks, core, scatter_dimension=0, tiled=True)
    return lax.psum_scatter(blocks, chips, scatter_dimension=0, tiled=True)[0]


def copy_for_each(value, axis):
    count = lax.axis_size(axis)
    return lax.all_to_all(
        jnp.broadcast_to(value[None], (count, *value.shape)), axis, 0, 0, tiled=True
    )


def of_everyone(value, axis):
    everything = copy_for_each(value, axis)
    return jnp.sum(everything.astype(jnp.float32), axis=0)


def taken_together(value, axis):
    everything = copy_for_each(value, axis)
    return jnp.sum(everything, axis=0)


def whole_sweeps(matrix, column_width, groups_all, sweeps, scale):
    hidden_width = matrix.shape[0]
    group = math.gcd(8, groups_all)
    current = matrix
    result = None
    for sweep in range(sweeps):

        def add_group(index, total):
            cols = lax.dynamic_slice_in_dim(
                current, index * group * column_width, group * column_width, 1
            )
            cols = cols.reshape(hidden_width, group, column_width)
            term = jnp.einsum(
                "fnd,gnd->nfg", cols, cols, preferred_element_type=jnp.float32
            ).astype(jnp.bfloat16)
            return total + jnp.sum(lax.optimization_barrier(term).astype(jnp.float32), axis=0)

        gram = lax.fori_loop(
            0, groups_all // group, add_group, jnp.zeros((hidden_width, hidden_width), jnp.float32)
        )
        gram_half = gram.astype(jnp.bfloat16)
        squared = jnp.dot(gram_half, gram_half, preferred_element_type=jnp.float32)
        poly = (ns_second * gram + ns_third * squared).astype(jnp.bfloat16)
        newer = ns_first * current.astype(jnp.float32) + jnp.dot(
            poly, current, preferred_element_type=jnp.float32
        )
        if sweep + 1 < sweeps:
            current = newer.astype(jnp.bfloat16)
        else:
            result = (scale * newer).astype(jnp.bfloat16)
    return result


def per_device(
    token_inputs, cotangent, gate_preact, up_preact, down_weight, block_expert, block_count
):
    blocks = block_count.shape[0]
    rows_here = token_inputs.shape[0]
    hidden_width = gate_preact.shape[1]
    width = token_inputs.shape[1]
    block_rows = rows_here // blocks
    experts_here = down_weight.shape[0]
    row_place = jnp.arange(rows_here, dtype=jnp.int32) % block_rows
    row_count = jnp.repeat(block_count, block_rows, total_repeat_length=rows_here)
    row_expert = jnp.repeat(block_expert, block_rows, total_repeat_length=rows_here)
    live_rows = row_place < row_count
    masked = jnp.where(live_rows[:, None], cotangent, jnp.zeros_like(cotangent))
    gate = gate_preact.astype(jnp.float32)
    upper = up_preact.astype(jnp.float32)
    sigmoid_gate = jax.nn.sigmoid(gate)
    hidden = (gate * sigmoid_gate * upper).astype(jnp.bfloat16)
    selector = (row_expert[None, :] == jnp.arange(experts_here, dtype=jnp.int32)[:, None]).astype(
        jnp.bfloat16
    )
    masked_each = masked[None, :, :] * selector[:, :, None]
    weights_all = lax.all_gather(down_weight, DP, axis=2, tiled=True)
    back = jnp.einsum("erd,efd->rf", masked_each, weights_all, preferred_element_type=jnp.float32)
    grad_gate = (back * upper * sigmoid_gate * (1.0 + gate * (1.0 - sigmoid_gate))).astype(
        jnp.bfloat16
    )
    grad_up = (back * gate * sigmoid_gate).astype(jnp.bfloat16)
    gate_up = jnp.concatenate([grad_gate, grad_up], axis=1)
    gate_up_each = gate_up[None, :, :] * selector[:, :, None]
    hidden_each = hidden[None, :, :] * selector[:, :, None]
    input_part = jnp.einsum(
        "erf,rd->efd", gate_up_each, token_inputs, preferred_element_type=jnp.float32
    )
    output_part = jnp.einsum("erf,rd->efd", hidden_each, masked, preferred_element_type=jnp.float32)
    partial_value = jnp.concatenate(
        [input_part.reshape(experts_here, 2, hidden_width, width), output_part[:, None]], axis=1
    )
    partial_half = partial_value.astype(jnp.bfloat16)
    terms = lax.optimization_barrier(partial_half).astype(jnp.float32)
    grad = sum_by_chip(terms.astype(jnp.bfloat16), ("dp_0", "dp_1"), "dp_2", 3).astype(jnp.float32)
    grad = of_everyone(grad.astype(jnp.bfloat16), "rep").astype(jnp.float32)
    squares = taken_together(jnp.sum(grad * grad, axis=(2, 3)), DP)
    current = (grad / (jnp.sqrt(squares) + norm_eps)[:, :, None, None]).astype(jnp.bfloat16)
    column_width = current.shape[3]
    scale = jnp.sqrt(jnp.float32(D))
    result = None
    n_dp = lax.axis_size(DP)
    matrices = experts_here * 3
    flat = current.reshape(matrices, hidden_width, column_width)
    padding = jnp.zeros((n_dp - matrices, hidden_width, column_width), jnp.bfloat16)
    outbound = jnp.concatenate([flat, padding], axis=0)
    owned = lax.all_to_all(outbound, DP, split_axis=0, concat_axis=2, tiled=True)
    finished = whole_sweeps(owned[0], column_width, n_dp, ITERS, scale)
    returned = lax.all_to_all(finished[None], DP, split_axis=2, concat_axis=0, tiled=True)
    result = returned[:matrices].reshape(experts_here, 3, hidden_width, column_width)
    return result


def solution(mesh):
    torus = Mesh(mesh.devices.reshape(4, 4, 2, mesh.shape["rep"]), ("dp_0", "dp_1", "dp_2", "rep"))
    return jax.shard_map(
        per_device,
        mesh=torus,
        in_specs=(
            P(DP_REP, None),
            P(DP_REP, None),
            P(DP_REP, None),
            P(DP_REP, None),
            P(None, None, DP),
            P(DP_REP),
            P(DP_REP),
        ),
        out_specs=P(None, None, None, DP),
        check_vma=False,
    )
```

profile of v0, /device:TPU:1, one launch (start us, length us, event | category | flops | bytes accessed | tf_op | source)
XLA Modules:
  0.0 566.8 jit_solution(1773095210929279019)
XLA Ops:
  18.3 44.0 %all-gather.2.cloned.1.call-done = bf16[2,768,2048]{1,2,0:T(8,128)(2,1)} async-done(((bf16[2,768,64]{1,2,0:T(8,128)(2,1)}), bf16[2,768,2048]{1,2,0:T(8,128)(2,1)}) %all-gather.2.cloned.1.call-update) | async-done | bytes 6291472 | tf_op jit(solution)/shard_map/all_gather | solution.py:108
  62.4 7.8 %fusion.10 = (bf16[512,768]{1,0:T(8,128)(2,1)S(1)}, bf16[512,768]{1,0:T(8,128)(2,1)S(1)}, bf16[512,768]{1,0:T(8,128)(2,1)S(1)}) fusion(bf16[512,768]{1,0:T(8,128)(2,1)} %param.20, bf16[512,768]{1,0:T(8,128)(2,1)} %param.19, bf16[2,768,2048]{1,2,0:T(8,128)(2,1)} %all-gather.2.cloned.1.call-done, bf16[2,512]{1,0:T(2,128)(2,1)S(1)} %compare_convert_fusion, ...), kind=kOutput, calls=%fused_computation.33 | convolution fusion | flops 3230400512 | bytes 12322816 | tf_op jit(solution)/shard_map/erd,efd->rf/dot_general | solution.py:109
  74.0 10.6 %convolution_convert_fusion.2 = bf16[2,1536,2048]{2,1,0:T(8,128)(2,1)} fusion(bf16[512,2048]{1,0:T(8,128)(2,1)S(1)} %copy-done, bf16[2,512]{1,0:T(2,128)(2,1)S(1)} %compare_convert_fusion, bf16[512,1536]{0,1:T(8,128)(2,1)} %copy.51), kind=kOutput, calls=%fused_computation.9 | convolution fusion | flops 6450315264 | bytes 16254976 | tf_op jit(solution)/shard_map/erf,rd->efd/dot_general | solution.py:117
  84.7 16.8 %copy.53 = bf16[2,2,768,2048]{2,3,1,0:T(8,128)(2,1)} copy(bf16[2,2,768,2048]{3,2,1,0:T(8,128)(2,1)} %bitcast.100) | data formatting | bytes 25165824 | tf_op jit(solution)/shard_map/reshape | solution.py:122
  102.6 6.3 %convert_bitcast_fusion = bf16[2,1,768,2048]{3,2,0,1:T(8,128)(2,1)} fusion(bf16[512,2048]{1,0:T(8,128)(2,1)S(1)} %copy-done.2, bf16[2,512]{1,0:T(2,128)(2,1)S(1)} %compare_convert_fusion, bf16[512,768]{0,1:T(8,128)(2,1)} %copy.52), kind=kOutput, calls=%fused_computation.12 | convolution fusion | flops 3225157632 | bytes 9177088 | tf_op jit(solution)/shard_map/erf,rd->efd/dot_general | solution.py:120
  108.9 8.7 %copy.54 = bf16[2,1,768,2048]{2,3,1,0:T(8,128)(2,1)} copy(bf16[2,1,768,2048]{3,2,0,1:T(8,128)(2,1)} %convert_bitcast_fusion) | data formatting | bytes 12582912 | tf_op jit(solution)/shard_map/broadcast_in_dim | solution.py:122
  117.6 9.5 %pad_maximum_fusion = bf16[2,3,768,2048]{2,3,1,0:T(8,128)(2,1)S(1)} fusion(bf16[2,1,768,2048]{2,3,1,0:T(8,128)(2,1)} %copy.54, bf16[2,2,768,2048]{2,3,1,0:T(8,128)(2,1)} %copy.53), kind=kLoop, calls=%fused_computation.8 | loop fusion | flops 9437184 | bytes 37748736 | tf_op jit(solution)/shard_map/concatenate | solution.py:121
  127.1 6.7 %copy.55 = bf16[16,2,2,3,768,64]{4,5,3,2,0,1:T(8,128)(2,1)} copy(bf16[16,2,2,3,768,64]{4,5,1,0,3,2:T(8,128)(2,1)S(1)} %bitcast.97) | data formatting | bytes 37748736 | tf_op jit(solution)/shard_map/reshape | solution.py:31
  133.9 28.0 %reduce-scatter.5.cloned.1.call-done = bf16[16,2,3,768,64]{3,4,2,1,0:T(8,128)(2,1)} async-done(((bf16[32,2,3,768,64]{3,4,2,1,0:T(8,128)(2,1)}), bf16[16,2,3,768,64]{3,4,2,1,0:T(8,128)(2,1)}) %reduce-scatter.5.cloned.1.call-update) | async-done | bytes 9437200 | tf_op jit(solution)/shard_map/reduce_scatter | solution.py:32
  161.9 91.3 %reduce-scatter.7.cloned.1.call-done = bf16[1,2,3,768,64]{3,4,2,1,0:T(8,128)(2,1)} async-done(((bf16[16,2,3,768,64]{3,4,2,1,0:T(8,128)(2,1)}), bf16[1,2,3,768,64]{3,4,2,1,0:T(8,128)(2,1)}) %reduce-scatter.7.cloned.1.call-update) | async-done | bytes 589840
  254.5 30.7 %all_to_all.40 = bf16[4,2,3,768,64]{3,4,2,1,0:T(8,128)(2,1)S(1)} all-to-all(bf16[4,2,3,768,64]{3,4,2,1,0:T(8,128)(2,1)S(1)} %broadcast_in_dim.31), channel_id=1, replica_groups=mesh['dp_0'=4,'dp_1'=4,'dp_2'=2,'rep'=4] {'rep'}, dimensions={0} | all-to-all | bytes 4718592 | tf_op jit(solution)/shard_map/all_to_all | solution.py:38
  285.8 15.0 %all_to_all.41 = f32[32,2,3]{2,1,0:T(2,128)S(1)} all-to-all(f32[32,2,3]{2,1,0:T(2,128)S(1)} %broadcast_in_dim.32), channel_id=1, replica_groups=mesh['dp_0'=4,'dp_1'=4,'dp_2'=2,'rep'=4] {'dp_0','dp_1','dp_2'}, dimensions={0} | all-to-all | bytes 1536 | tf_op jit(solution)/shard_map/all_to_all | solution.py:38
  303.3 5.0 all-to-all-start.2
  308.3 39.9 %all-to-all-done.2 = bf16[32,768,64]{1,2,0:T(8,128)(2,1)} async-done(((bf16[32,768,64]{1,2,0:T(8,128)(2,1)}), bf16[32,768,64]{1,2,0:T(8,128)(2,1)}, u32[]{:S(2)}, u32[]{:S(2)}) %all-to-all-start.2) | async-done | bytes 3145760 | tf_op jit(solution)/shard_map/all_to_all | solution.py:138
  348.2 4.7 copy.58
  352.9 33.6 %while.34 = (s32[]{:T(128)}, f32[768,768]{1,0:T(8,128)}, bf16[768,2048]{0,1:T(8,128)(2,1)}, s32[]{:T(128)}, s32[]{:T(128)}, /*index=5*/s32[]{:T(128)}, s32[]{:T(128)}) while((s32[]{:T(128)}, f32[768,768]{1,0:T(8,128)}, bf16[768,2048]{0,1:T(8,128)(2,1)}, s32[]{:T(128)}, s32[]{:T(128)}, /*index=5*/s32[]{:T(128)}, s32[]{:T(128)}) %tuple.98), condition=%wide.region_7.9_spmd.clone, body=%wide.region_5.8_spmd.clone.sunk | while | flops 618725376 | bytes 30670984 | solution.py:70
  386.5 10.5 %add_convert_fusion = bf16[768,2048]{1,0:T(8,128)(2,1)} fusion(bf16[768,2048]{1,0:T(8,128)(2,1)} %copy.58, bf16[768,2048]{0,1:T(8,128)(2,1)} %bitcast.23, f32[768,768]{1,0:T(8,128)} %get-tuple-element.202), kind=kOutput, calls=%fused_computation.11 | convolution fusion | flops 3331129344 | bytes 11796480 | tf_op jit(solution)/shard_map/dot_general | solution.py:76
  397.0 34.4 %while.35 = (s32[]{:T(128)}, f32[768,768]{1,0:T(8,128)}, bf16[768,2048]{1,0:T(8,128)(2,1)}, s32[]{:T(128)}, s32[]{:T(128)}, /*index=5*/s32[]{:T(128)}, s32[]{:T(128)}) while((s32[]{:T(128)}, f32[768,768]{1,0:T(8,128)}, bf16[768,2048]{1,0:T(8,128)(2,1)}, s32[]{:T(128)}, s32[]{:T(128)}, /*index=5*/s32[]{:T(128)}, s32[]{:T(128)}) %tuple.101), condition=%wide.region_10.12_spmd.clone, body=%wide.region_8.11_spmd.clone.sunk | while | flops 618725376 | bytes 32243848 | solution.py:70
  431.4 8.5 %fusion.3 = bf16[1,768,2048]{2,1,0:T(8,128)(2,1)S(1)} fusion(bf16[768,2048]{1,0:T(8,128)(2,1)} %get-tuple-element.360, f32[768,768]{1,0:T(8,128)} %get-tuple-element.203), kind=kOutput, calls=%fused_computation.17 | convolution fusion | flops 3332702208 | bytes 8650752 | tf_op jit(solution)/shard_map/dot_general | solution.py:76
  439.9 11.2 %copy.60 = bf16[1,768,2048]{1,0,2:T(2,128)(2,1)} copy(bf16[1,768,2048]{2,1,0:T(8,128)(2,1)S(1)} %fusion.3) | data formatting | bytes 6291456 | tf_op jit(solution)/shard_map/broadcast_in_dim | solution.py:140
  451.7 33.3 %reduce.3 = bf16[2048,768]{1,0:T(8,128)(2,1)} reduce(bf16[2048,1,768]{2,1,0:T(2,128)(2,1)} %bitcast.98, bf16[]{:T(256)} %broadcast.220), dimensions={1}, to_apply=%bitcast.73.reduce_sub_computation | reduce | bytes 6291458
  485.0 6.6 %reshape.174 = bf16[32,2,24576]{2,1,0:T(2,128)(2,1)S(1)} reshape(bf16[2048,768]{1,0:T(8,128)(2,1)} %reduce.3) | data formatting | bytes 6291456
  491.6 45.5 %all_to_all.42 = bf16[32,2,24576]{2,1,0:T(2,128)(2,1)} all-to-all(bf16[32,2,24576]{2,1,0:T(2,128)(2,1)S(1)} %reshape.174), channel_id=1, replica_groups=mesh['dp_0'=4,'dp_1'=4,'dp_2'=2,'rep'=4] {'dp_0','dp_1','dp_2'}, dimensions={0} | all-to-all | bytes 6291456 | tf_op jit(solution)/shard_map/all_to_all | solution.py:140
  537.1 18.9 %reshape.175 = bf16[2048,1,768]{2,1,0:T(2,128)(2,1)} reshape(bf16[32,2,24576]{2,1,0:T(2,128)(2,1)} %all_to_all.42) | data formatting | bytes 6291456
  (73 shorter events, 94.0 us)
Async XLA Ops:
  6.5 67.5 %copy-start = (bf16[512,2048]{1,0:T(8,128)(2,1)S(1)}, bf16[512,2048]{1,0:T(8,128)(2,1)}, u32[]{:S(2)}) copy-start(bf16[512,2048]{1,0:T(8,128)(2,1)} %param.17) | copy-start | bytes 6291460
  6.5 55.8 %all-gather.2.cloned.1.call-start = ((), (), s32[]{:S(2)}) async-start(), calls=%async_computation.6 | async-start | bytes 6488064 | tf_op jit(solution)/shard_map/all_gather | solution.py:108
  7.3 154.6 %reduce-scatter.5.cloned.1.call-start = ((), (), s32[]{:S(2)}) async-start(), calls=%async_computation.7 | async-start | bytes 28311552 | tf_op jit(solution)/shard_map/reduce_scatter | solution.py:32
  84.7 18.0 %copy-start.2 = (bf16[512,2048]{1,0:T(8,128)(2,1)S(1)}, bf16[512,2048]{1,0:T(8,128)(2,1)}, u32[]{:S(2)}) copy-start(bf16[512,2048]{1,0:T(8,128)(2,1)} %broadcast_select_fusion) | copy-start | bytes 6291460
  133.8 119.4 %reduce-scatter.7.cloned.1.call-start = ((), (), s32[]{:S(2)}) async-start(), calls=%async_computation.8 | async-start | bytes 10027008
  303.3 44.9 %all-to-all-start.2 = ((bf16[32,768,64]{1,2,0:T(8,128)(2,1)}), bf16[32,768,64]{1,2,0:T(8,128)(2,1)}, u32[]{:S(2)}, u32[]{:S(2)}) async-start(bf16[32,768,64]{1,2,0:T(8,128)(2,1)} %concatenate.18), calls=%async_computation.3 | async-start | bytes 6291456 | tf_op jit(solution)/shard_map/all_to_all | solution.py:138
  556.0 4.3 copy-start.1
Sparse Core Ops, SparseCore 0:
  9.6 52.6 all-gather.1
  133.9 27.9 reduce-scatter.4
  165.4 87.7 reduce-scatter.6
where the time goes:
time: 570 us; the launch traced here: 567 us
  waiting for transfers between devices  204 us (36%)
  local copies, waits for them, and re-layouts  99.3 us (17%)
  blocking collectives  91.1 us (16%)
  other arithmetic  87 us (15%)
  matrix products  66.9 us (12%)
  between operations  13.2 us (2%)
    unnamed x4, waiting for transfers between devices  92 us
    all_to_all x2, blocking collectives, copy_for_each(): lax.all_to_all(jnp.broadcast_to(value[None], (count, *value.shape)), axis...  45.6 us
    all_to_all x1, blocking collectives, per_device(): lax.all_to_all(finished[None], DP, split_axis=2, concat_axis=0, tiled=True)  45.5 us
    all_gather x1, waiting for transfers between devices, per_device(): weights_all = lax.all_gather(down_weight, DP, axis=2, tiled=True)  44 us
    all_to_all x1, waiting for transfers between devices, per_device(): lax.all_to_all(outbound, DP, split_axis=0, concat_axis=2, tiled=True)  39.9 us
    unnamed x3, other arithmetic  33.3 us
    unnamed x11, local copies, waits for them, and re-layouts  29.6 us
    reduce_scatter x1, waiting for transfers between devices, sum_by_chip(): blocks = lax.psum_scatter(blocks, core, scatter_dimension=0, tiled=True)  28 us
  transfers between devices with their start and end apart: 4, of which 4 were waited for; matrix products, arithmetic and copies ran while one was open for 2% of the time, Pallas kernels for 0%

commit v1 on v0

v1 whole, which is shorter than its diff:
```python
import functools

import jax
import jax.numpy as jnp
from jax import lax
from jax.experimental import pallas as pl
from jax.experimental.pallas import tpu as pltpu
from jax.sharding import Mesh
from jax.sharding import PartitionSpec as P

D = 2048
F = 768
ROWS = 512
HALF = F // 2
THIRD = HALF // 2
LANES = 128
AXES = ("z", "x", "y")
ORDERS = (("z", "x", "y"), ("x", "y", "z"), ("y", "z", "x"))
MESH = pl.DeviceIdType.MESH

ns_first = 3.4445
ns_second = -4.775
ns_third = 2.0315
norm_eps = 1e-07

bf16 = jnp.bfloat16
f32 = jnp.float32


def around(axis):
    i = lax.axis_index(axis)
    return i, lax.rem(i + 1, 4), lax.rem(i + 3, 4), lax.rem(i + 2, 4)


def push(src, dst, send, recv, device):
    copy = pltpu.make_async_remote_copy(
        src_ref=src, dst_ref=dst, send_sem=send, recv_sem=recv, device_id=device, device_id_type=MESH
    )
    copy.start()
    return copy


def greet(axes, with_core):
    barrier = pltpu.get_barrier_semaphore()
    count = 0
    for axis in axes:
        i, right, left, far = around(axis)
        for other in (right, left):
            pl.semaphore_signal(barrier, inc=1, device_id={axis: other}, device_id_type=MESH)
            count += 1
    if with_core:
        c = lax.axis_index("core")
        pl.semaphore_signal(barrier, inc=1, device_id={"core": 1 - c}, device_id_type=MESH)
        count += 1
    pl.semaphore_wait(barrier, count)


class Scatter:
    def __init__(self, axis, src, first, second, near, final, send, recv, add):
        self.axis, self.src, self.first, self.second = axis, src, first, second
        self.near, self.final, self.send, self.recv, self.add = near, final, send, recv, add

    def start(self):
        i, right, left, far = around(self.axis)
        src, first, second, send, recv = self.src, self.first, self.second, self.send, self.recv
        to_right, to_left = {self.axis: right}, {self.axis: left}
        self.a1 = push(first(src.at[far]), first(self.near), send.at[0], recv.at[0], to_right)
        self.b1 = push(second(src.at[far]), second(self.near), send.at[1], recv.at[1], to_left)
        self.a2 = push(second(src.at[right]), second(self.final.at[0]), send.at[2], recv.at[2], to_right)
        self.b2 = push(first(src.at[left]), first(self.final.at[1]), send.at[3], recv.at[3], to_left)

    def middle(self):
        i, right, left, far = around(self.axis)
        src, first, second, send, recv = self.src, self.first, self.second, self.send, self.recv
        self.a1.wait_recv()
        self.add(first(src.at[right]), (first(self.near),))
        self.a3 = push(first(src.at[right]), first(self.final.at[0]), send.at[4], recv.at[4], {self.axis: right})
        self.b1.wait_recv()
        self.add(second(src.at[left]), (second(self.near),))
        self.b3 = push(second(src.at[left]), second(self.final.at[1]), send.at[5], recv.at[5], {self.axis: left})

    def finish(self):
        i, right, left, far = around(self.axis)
        for copy in (self.a2, self.b2, self.a3, self.b3):
            copy.wait_recv()
        self.add(self.src.at[i], (self.final.at[0], self.final.at[1]))

    def drain(self):
        for copy in (self.a1, self.b1, self.a2, self.b2, self.a3, self.b3):
            copy.wait_send()


class Gather:
    def __init__(self, axis, buf, first, second, send, recv):
        self.axis, self.buf, self.first, self.second = axis, buf, first, second
        self.send, self.recv = send, recv

    def start(self):
        i, right, left, far = around(self.axis)
        buf = self.buf
        self.a1 = push(buf.at[i], buf.at[i], self.send.at[0], self.recv.at[0], {self.axis: right})
        self.b1 = push(buf.at[i], buf.at[i], self.send.at[1], self.recv.at[1], {self.axis: left})

    def middle(self):
        i, right, left, far = around(self.axis)
        buf, first, second = self.buf, self.first, self.second
        self.a1.wait_recv()
        self.a2 = push(first(buf.at[left]), first(buf.at[left]), self.send.at[2], self.recv.at[2], {self.axis: right})
        self.b1.wait_recv()
        self.b2 = push(second(buf.at[right]), second(buf.at[right]), self.send.at[3], self.recv.at[3], {self.axis: left})

    def finish(self):
        self.a2.wait_recv()
        self.b2.wait_recv()

    def drain(self):
        for copy in (self.a1, self.b1, self.a2, self.b2):
            copy.wait_send()


def add_blocks(dst, others):
    lead = dst.shape[:-2]
    count = 1
    for size in lead:
        count *= size

    def one(n, carry):
        index = []
        rest = n
        for size in reversed(lead):
            index.append(lax.rem(rest, size))
            rest = lax.div(rest, size)
        index = tuple(reversed(index))
        total = dst[index].astype(f32)
        for other in others:
            total = total + other[index].astype(f32)
        dst[index] = total.astype(bf16)
        return carry

    if count == 1:
        one(0, 0)
    else:
        lax.fori_loop(0, count, one, 0)


def lead_halves(size):
    half = size // 2
    return (lambda ref: ref.at[pl.ds(0, half)]), (lambda ref: ref.at[pl.ds(half, half)])


def lane_halves(size, cut):
    return (lambda ref: ref.at[:, pl.ds(0, cut)]), (lambda ref: ref.at[:, pl.ds(cut, size - cut)])


def grad_kernel(
    masked, tokens, gate_t, up_t, row_expert, w_pad, out,
    mk, tk, gb, ub, rex, wx, wall, left_side, part,
    near0, fin0, near1, fin1, near2, fin2,
    own_sem, x_send, x_recv, w_send, w_recv, r_send, r_recv,
):
    c = lax.axis_index("core")
    other = {"core": 1 - c}
    sources = (w_pad.at[c], gate_t.at[c], up_t.at[c], row_expert, masked, tokens)
    gives = (w_pad.at[1 - c], gate_t.at[1 - c], up_t.at[1 - c], row_expert, masked, tokens)
    places = (wx, gb, ub, rex, mk, tk)
    own = []
    for n in range(6):
        copy = pltpu.make_async_copy(sources[n], places[n].at[0], own_sem.at[n])
        copy.start()
        own.append(copy)
    greet(AXES, True)
    cross = [
        push(gives[n], places[n].at[1], x_send.at[n], x_recv.at[n], other) for n in range(6)
    ]

    def ready(n):
        own[n].wait()
        cross[n].wait_recv()

    z, x = lax.axis_index("z"), lax.axis_index("x")
    first, second = lead_halves(HALF)
    four_first, four_second = lead_halves(4)
    w_near = [
        Gather("z", wall.at[0, x], first, second, w_send.at[0], w_recv.at[0]),
        Gather("x", wall.at[1, z], first, second, w_send.at[1], w_recv.at[1]),
    ]
    w_far = [
        Gather("x", wall.at[0], four_first, four_second, w_send.at[2], w_recv.at[2]),
        Gather("z", wall.at[1], four_first, four_second, w_send.at[3], w_recv.at[3]),
    ]
    ready(0)
    wall[0, x, z] = wx[0, 0] + wx[1, 0]
    wall[1, z, x] = wx[0, 1] + wx[1, 1]
    for one in w_near:
        one.start()

    rs = []
    cut0, cut1, cut2 = lead_halves(4), lead_halves(4), lead_halves(THIRD)
    for k in range(3):
        order = ORDERS[k]
        a, b = lax.axis_index(order[0]), lax.axis_index(order[1])
        rs.append(
            (
                Scatter(order[0], part.at[k], *cut0, near0.at[k], fin0.at[k], r_send.at[k, 0], r_recv.at[k, 0], add_blocks),
                Scatter(order[1], part.at[k, a], *cut1, near1.at[k], fin1.at[k], r_send.at[k, 1], r_recv.at[k, 1], add_blocks),
                Scatter(order[2], part.at[k, a, b], *cut2, near2.at[k], fin2.at[k], r_send.at[k, 2], r_recv.at[k, 2], add_blocks),
            )
        )

    for n in (1, 2, 3):
        ready(n)
    tile = 32
    for s in range(2):
        @pl.loop(0, HALF // tile)
        def hidden_rows(t, s=s):
            rows = pl.ds(pl.multiple_of(t * tile, tile), tile)
            gate = gb[s, rows, :].astype(f32)
            upper = ub[s, rows, :].astype(f32)
            hidden = gate * jax.nn.sigmoid(gate) * upper
            which = rex[s, 0:1, :]
            half = lax.div(t, THIRD // tile)
            place = pl.ds(pl.multiple_of(lax.rem(t, THIRD // tile) * tile, tile), tile)
            for e in range(2):
                kept = jnp.where(which == e, hidden, 0.0).astype(bf16)
                left_side[2, 2 * e + half, place, s * ROWS:(s + 1) * ROWS] = kept

    for one in w_near:
        one.middle()

    def products(k, right):
        lhs = left_side.at[k]

        @pl.loop(0, 4)
        def columns(iz):
            cols = pl.ds(pl.multiple_of(iz * 512, 512), 512)
            r0, r1 = right[0, :, cols], right[1, :, cols]
            for y in range(4):
                acc = jnp.dot(lhs[y, :, 0:ROWS], r0, preferred_element_type=f32)
                acc = acc + jnp.dot(lhs[y, :, ROWS:], r1, preferred_element_type=f32)
                acc = acc.astype(bf16)
                for ix in range(4):
                    where = {"z": iz, "x": ix, "y": y}
                    index = tuple(where[axis] for axis in ORDERS[k])
                    part[(k,) + index] = acc[:, ix * LANES:(ix + 1) * LANES]

    for one in w_near:
        one.finish()
    for one in w_far:
        one.start()
    ready(4)
    products(2, mk)
    rs[2][0].start()
    for one in w_far:
        one.middle()
    for one in w_far:
        one.finish()

    for s in range(2):
        @pl.loop(0, 4)
        def back_rows(t, s=s):
            k, sub = lax.div(t, 2), lax.rem(t, 2)
            rows = pl.ds(pl.multiple_of(t * 96, 96), 96)
            place = pl.ds(pl.multiple_of(sub * 96, 96), 96)
            which = rex[s, 0:1, :]
            right = mk[s]
            both = []
            for e in range(2):
                pieces = []
                for iz in range(4):
                    for ix in range(4):
                        pieces.append(wall[0, ix, iz, rows, :] if e == 0 else wall[1, iz, ix, rows, :])
                w = jnp.concatenate(pieces, axis=1)
                both.append(lax.dot_general(w, right, (((1,), (1,)), ((), ())), preferred_element_type=f32))
            back = jnp.where(which == 0, both[0], both[1])
            gate = gb[s, rows, :].astype(f32)
            upper = ub[s, rows, :].astype(f32)
            sig = jax.nn.sigmoid(gate)
            grads = (back * upper * sig * (1.0 + gate * (1.0 - sig)), back * gate * sig)
            for e in range(2):
                for h in range(2):
                    kept = jnp.where(which == e, grads[h], 0.0).astype(bf16)
                    left_side[k, 2 * e + h, place, s * ROWS:(s + 1) * ROWS] = kept

    ready(5)
    products(0, tk)
    rs[0][0].start()
    rs[2][0].middle()
    products(1, tk)
    rs[1][0].start()
    rs[2][0].finish()
    rs[2][1].start()
    rs[0][0].middle()
    rs[1][0].middle()
    rs[2][1].middle()
    rs[2][1].finish()
    rs[2][2].start()
    rs[2][2].middle()
    rs[2][2].finish()
    rs[0][0].finish()
    rs[0][1].start()
    rs[1][0].finish()
    rs[1][1].start()
    rs[0][1].middle()
    rs[1][1].middle()
    rs[0][1].finish()
    rs[0][2].start()
    rs[1][1].finish()
    rs[1][2].start()
    rs[0][2].middle()
    rs[1][2].middle()
    rs[0][2].finish()
    rs[1][2].finish()
    for k in range(3):
        order = ORDERS[k]
        a, b, d = (lax.axis_index(axis) for axis in order)
        out[k] = part[k, a, b, d]
    for copy in cross:
        copy.wait_send()
    for one in w_near + w_far:
        one.drain()
    for k in range(3):
        for one in rs[k]:
            one.drain()


def grad_sums(masked, tokens, gate_t, up_t, row_expert, w_pad):
    anywhere = pl.BlockSpec(memory_space=pl.ANY)
    vmem = pltpu.VMEM
    dma = pltpu.SemaphoreType.DMA
    return pl.pallas_call(
        grad_kernel,
        out_shape=jax.ShapeDtypeStruct((3, THIRD, LANES), bf16),
        in_specs=[anywhere] * 6,
        out_specs=pl.BlockSpec(memory_space=vmem),
        scratch_shapes=[
            vmem((2, ROWS, D), bf16),
            vmem((2, ROWS, D), bf16),
            vmem((2, HALF, ROWS), bf16),
            vmem((2, HALF, ROWS), bf16),
            vmem((2, 8, ROWS), f32),
            vmem((2, 2, HALF, LANES), bf16),
            vmem((2, 4, 4, HALF, LANES), bf16),
            vmem((3, 4, THIRD, 2 * ROWS), bf16),
            vmem((3, 4, 4, 4, THIRD, LANES), bf16),
            vmem((3, 4, 4, THIRD, LANES), bf16),
            vmem((3, 2, 4, 4, THIRD, LANES), bf16),
            vmem((3, 4, THIRD, LANES), bf16),
            vmem((3, 2, 4, THIRD, LANES), bf16),
            vmem((3, THIRD, LANES), bf16),
            vmem((3, 2, THIRD, LANES), bf16),
            dma((6,)),
            dma((6,)),
            dma((6,)),
            dma((4, 4)),
            dma((4, 4)),
            dma((3, 3, 6)),
            dma((3, 3, 6)),
        ],
        compiler_params=pltpu.CompilerParams(
            collective_id=0, has_side_effects=True, vmem_limit_bytes=60 * 1024 * 1024
        ),
        name="grad_sums",
    )(masked, tokens, gate_t, up_t, row_expert, w_pad)


GRAM_ROWS = F // 16


def newton_kernel(
    sums, out,
    pair, from_core, pair_core, mat, gram, whole, near0, fin0, near1, fin1,
    g1, p1, u, g2, p2,
    x_send, x_recv, g_send, g_recv, a_send, a_recv, o_send, o_recv,
):
    c, y = lax.axis_index("core"), lax.axis_index("y")
    h = lax.rem(y, 2)
    mate = y + 1 - 2 * h
    other = {"core": 1 - c}
    greet(AXES, True)
    down = push(sums.at[2], pair, x_send.at[0], x_recv.at[0], {"y": mate})
    swap = push(sums, from_core, x_send.at[1], x_recv.at[1], other)
    down.wait_recv()
    onward = push(pair, pair_core, x_send.at[2], x_recv.at[2], other)
    swap.wait_recv()
    onward.wait_recv()

    @pl.when(c == 0)
    def first_core():
        for k in range(2):
            mat[k] = sums[k]
            mat[2 + k] = from_core[k]

    @pl.when(c == 1)
    def second_core():
        mat[h] = from_core[2]
        mat[1 - h] = pair_core[...]
        mat[2 + h] = sums[2]
        mat[3 - h] = pair[...]

    X = jnp.concatenate([mat[k] for k in range(4)], axis=0)
    for a in range(4):
        block = lax.dot_general(mat[a], X, (((1,), (1,)), ((), ())), preferred_element_type=f32).astype(bf16)
        for b in range(4):
            for k in range(2):
                gram[k, a, b] = block[b * GRAM_ROWS:(b + 1) * GRAM_ROWS, k * HALF:(k + 1) * HALF]

    four = lead_halves(4)
    lanes = lane_halves(HALF, LANES)
    orders = (("z", "x"), ("x", "z"))
    rs0, rs1, ag0, ag1 = [], [], [], []
    for k in range(2):
        first_axis, second_axis = orders[k]
        a = lax.axis_index(first_axis)
        rs0.append(Scatter(first_axis, gram.at[k], *four, near0.at[k], fin0.at[k], g_send.at[k, 0], g_recv.at[k, 0], add_blocks))
        rs1.append(Scatter(second_axis, gram.at[k, a], *lanes, near1.at[k], fin1.at[k], g_send.at[k, 1], g_recv.at[k, 1], add_blocks))
        ag0.append(Gather(second_axis, whole.at[k, a], *lanes, a_send.at[k, 0], a_recv.at[k, 0]))
        ag1.append(Gather(first_axis, whole.at[k], *four, a_send.at[k, 1], a_recv.at[k, 1]))
    for k in range(2):
        rs0[k].start()
    for k in range(2):
        rs0[k].middle()
    for k in range(2):
        rs0[k].finish()
        rs1[k].start()
    for k in range(2):
        rs1[k].middle()
    for k in range(2):
        rs1[k].finish()
        a, b = (lax.axis_index(axis) for axis in orders[k])
        whole[k, a, b] = gram[k, a, b]
        ag0[k].start()
    for k in range(2):
        ag0[k].middle()
    for k in range(2):
        ag0[k].finish()
        ag1[k].start()
    for k in range(2):
        ag1[k].middle()
    for k in range(2):
        ag1[k].finish()

    trace = jnp.zeros((GRAM_ROWS, HALF), f32)
    row = lax.broadcasted_iota(jnp.int32, (GRAM_ROWS, HALF), 0)
    col = lax.broadcasted_iota(jnp.int32, (GRAM_ROWS, HALF), 1)
    for n in range(16):
        k, start = n // 8, (n % 8) * GRAM_ROWS
        trace = trace + jnp.where(col == row + start, whole[k, n // 4, n % 4].astype(f32), 0.0)
    squares = jnp.sum(jnp.sum(trace, axis=0, keepdims=True), axis=1, keepdims=True)
    scale = 1.0 / (jnp.sqrt(squares) + norm_eps)
    for n in range(16):
        for k in range(2):
            value = whole[k, n // 4, n % 4].astype(f32) * scale * scale
            g1[n * GRAM_ROWS:(n + 1) * GRAM_ROWS, k * HALF:(k + 1) * HALF] = value.astype(bf16)

    def rowwise(body):
        @pl.loop(0, 3)
        def one(t):
            body(pl.ds(pl.multiple_of(t * 256, 256), 256))

    def times(left, right):
        return jnp.dot(left, right[...], preferred_element_type=f32)

    def make_p1(rows):
        g = g1[rows, :]
        p1[rows, :] = (ns_second * g.astype(f32) + ns_third * times(g, g1)).astype(bf16)

    def make_u(rows):
        u[rows, :] = (ns_first * g1[rows, :].astype(f32) + times(p1[rows, :], g1)).astype(bf16)

    def make_g2(rows):
        g2[rows, :] = (ns_first * u[rows, :].astype(f32) + times(p1[rows, :], u)).astype(bf16)

    def make_p2(rows):
        g = g2[rows, :]
        p2[rows, :] = (ns_second * g.astype(f32) + ns_third * times(g, g2)).astype(bf16)

    factor = scale * jnp.sqrt(f32(D))

    def make_out(rows):
        p = p2[rows, :]
        r = ns_first * (p1[rows, :].astype(f32) + p.astype(f32)) + times(p, p1)
        u[rows, :] = r.astype(bf16)

    for body in (make_p1, make_u, make_g2, make_p2, make_out):
        rowwise(body)
    for n in range(4):
        rows = pl.ds(n * THIRD, THIRD)
        new = ns_first * ns_first * mat[n].astype(f32) + jnp.dot(u[rows, :], X, preferred_element_type=f32)
        out[c, y, rows, :] = (factor * new).astype(bf16)

    halves = lead_halves(F)
    ring = Gather("y", out.at[c], *halves, o_send.at[0], o_recv.at[0])
    i, right, left, far = around("y")
    over = [push(out.at[c, i], out.at[c, i], x_send.at[3], x_recv.at[3], other)]
    ring.start()
    ring.middle()
    over.append(push(out.at[c, left], out.at[c, left], x_send.at[4], x_recv.at[4], other))
    over.append(push(out.at[c, right], out.at[c, right], x_send.at[5], x_recv.at[5], other))
    ring.finish()
    over.append(push(out.at[c, far], out.at[c, far], x_send.at[6], x_recv.at[6], other))
    for copy in over:
        copy.wait_recv()
    for copy in [down, swap, onward] + over:
        copy.wait_send()
    for one in rs0 + rs1 + ag0 + ag1 + [ring]:
        one.drain()


def newton(sums):
    vmem = pltpu.VMEM
    dma = pltpu.SemaphoreType.DMA
    square = vmem((F, F), bf16)
    return pl.pallas_call(
        newton_kernel,
        out_shape=jax.ShapeDtypeStruct((2, 4, F, LANES), bf16),
        in_specs=[pl.BlockSpec(memory_space=vmem)],
        out_specs=pl.BlockSpec(memory_space=vmem),
        scratch_shapes=[
            vmem((THIRD, LANES), bf16),
            vmem((3, THIRD, LANES), bf16),
            vmem((THIRD, LANES), bf16),
            vmem((4, THIRD, LANES), bf16),
            vmem((2, 4, 4, GRAM_ROWS, HALF), bf16),
            vmem((2, 4, 4, GRAM_ROWS, HALF), bf16),
            vmem((2, 4, GRAM_ROWS, HALF), bf16),
            vmem((2, 2, 4, GRAM_ROWS, HALF), bf16),
            vmem((2, GRAM_ROWS, HALF), bf16),
            vmem((2, 2, GRAM_ROWS, HALF), bf16),
            square, square, square, square, square,
            dma((7,)),
            dma((7,)),
            dma((2, 2, 6)),
            dma((2, 2, 6)),
            dma((2, 2, 4)),
            dma((2, 2, 4)),
            dma((1, 4)),
            dma((1, 4)),
        ],
        compiler_params=pltpu.CompilerParams(
            collective_id=1, has_side_effects=True, vmem_limit_bytes=60 * 1024 * 1024
        ),
        name="newton",
    )(sums)


def per_device(
    token_inputs, cotangent, gate_preact, up_preact, down_weight, block_expert, block_count
):
    blocks = block_count.shape[0]
    rows_here = token_inputs.shape[0]
    block_rows = rows_here // blocks
    c = lax.axis_index("core")
    row_place = jnp.arange(rows_here, dtype=jnp.int32) % block_rows
    row_count = jnp.repeat(block_count, block_rows, total_repeat_length=rows_here)
    masked = jnp.where((row_place < row_count)[:, None], cotangent, jnp.zeros_like(cotangent))
    row_expert = jnp.repeat(block_expert, block_rows, total_repeat_length=rows_here).astype(f32)
    row_expert = jnp.broadcast_to(row_expert[None, :], (8, rows_here))
    gate_t = gate_preact.T.reshape(2, HALF, rows_here)
    up_t = up_preact.T.reshape(2, HALF, rows_here)
    cols = down_weight.shape[2]
    lane = jnp.arange(2 * cols, dtype=jnp.int32) // cols
    w_pad = jnp.concatenate([down_weight, down_weight], axis=2)
    w_pad = jnp.where(lane[None, None, :] == c, w_pad, jnp.zeros_like(w_pad))
    w_pad = w_pad.reshape(2, 2, HALF, 2 * cols).swapaxes(0, 1)
    sums = grad_sums(masked, token_inputs, gate_t, up_t, row_expert, w_pad)
    done = newton(sums)
    mine = lax.dynamic_slice_in_dim(done, c * cols, cols, 3)
    top = mine[0].reshape(2, 2, F, cols)
    low = mine[1].reshape(2, 2, F, cols)[:, :1]
    return jnp.concatenate([top, low], axis=1)


def solution(mesh):
    torus = Mesh(mesh.devices.reshape(4, 4, 2, mesh.shape["rep"]), ("z", "x", "core", "y"))
    dp, dp_rep = ("z", "x", "core"), ("z", "x", "core", "y")
    return jax.shard_map(
        per_device,
        mesh=torus,
        in_specs=(
            P(dp_rep, None),
            P(dp_rep, None),
            P(dp_rep, None),
            P(dp_rep, None),
            P(None, None, dp),
            P(dp_rep),
            P(dp_rep),
        ),
        out_specs=P(None, None, None, dp),
        check_vma=False,
    )
```

time: 570 us -> 183 us (0.32)
  waiting for transfers between devices: 204 us -> 0 us
  Pallas kernels: 0 us -> 165 us
  local copies, waits for them, and re-layouts: 99.3 us -> 7.74 us
  blocking collectives: 91.1 us -> 0 us
  other arithmetic: 87 us -> 10.3 us
  matrix products: 66.9 us -> 0 us
  between operations: 13.2 us -> 0.1 us
    pallas_call x0 -> x2, Pallas kernels: none -> 165 us  [the longest x1 99.4 us: grad_sums(): pl.pallas_call(grad_kernel, out_shape=jax.ShapeDtypeStruct((3, THIRD, LAN...]
    unnamed x4 -> x0, waiting for transfers between devices: 92 us -> none
    all_to_all x3 -> x0, blocking collectives: 91.1 us -> none  [the longest x2 45.6 us: copy_for_each(): lax.all_to_all(jnp.broadcast_to(value[None], (count, *value.shape)), axis...]
    dot_general x13 -> x0, matrix products: 66.9 us -> none  [the longest x8 23.3 us: add_group(): jnp.einsum('fnd,gnd->nfg', cols, cols, preferred_element_type=jnp.float32)]
    all_gather x1 -> x0, waiting for transfers between devices: 44 us -> none  [per_device(): weights_all = lax.all_gather(down_weight, DP, axis=2, tiled=True)]
    all_to_all x1 -> x0, waiting for transfers between devices: 39.9 us -> none  [per_device(): lax.all_to_all(outbound, DP, split_axis=0, concat_axis=2, tiled=True)]
    unnamed x3 -> x0, other arithmetic: 33.3 us -> none
    unnamed x11 -> x9, local copies, waits for them, and re-layouts: 29.6 us -> 0.18 us
  transfers between devices with their start and end apart: 4 -> 0, of which waited for: 4 -> 0; matrix products, arithmetic and copies ran while one was open for 2% -> 0% of each run, Pallas kernels for 0% -> 0%
where the time goes in v1:
time: 183 us
  Pallas kernels  165 us (90%)
  other arithmetic  10.3 us (6%)
  local copies, waits for them, and re-layouts  7.74 us (4%)
    pallas_call x1, Pallas kernels, grad_sums(): pl.pallas_call(grad_kernel, out_shape=jax.ShapeDtypeStruct((3, THIRD, LAN...  99.4 us
    pallas_call x1, Pallas kernels, newton(): pl.pallas_call(newton_kernel, out_shape=jax.ShapeDtypeStruct((2, 4, F, LA...  65.5 us

profile of v1, /device:TPU:1, one launch (start us, length us, event | category | flops | bytes accessed | tf_op | source)
XLA Modules:
  0.0 183.0 jit_solution(5553635626031153587)
XLA Ops:
  0.0 1.5 fusion.10
  1.5 2.6 %fusion.1 = pred[512]{0:T(512)(128)(4,1)S(1)} fusion(s32[]{:T(128)} %bitcast.4, s32[]{:T(128)} %bitcast.3, s32[]{:T(128)} %bitcast.2, s32[]{:T(128)} %bitcast.1), kind=kLoop, calls=%fused_computation.6 | loop fusion | flops 11264 | bytes 528 | tf_op jit(solution)/shard_map/lt | solution.py:555
  4.1 0.0 copy-start.3
  4.1 0.0 copy-start.2
  4.1 0.0 copy-start
  4.1 3.2 %broadcast_select_fusion.masked = bf16[512,2048]{1,0:T(8,128)(2,1)} fusion(bf16[512,2048]{1,0:T(8,128)(2,1)} %param.14, pred[512]{0:T(512)(128)(4,1)S(1)} %fusion.1), kind=kLoop, calls=%fused_computation | loop fusion | flops 1048576 | bytes 4194816 | tf_op jit(solution)/shard_map/jit(_where)/select_n | solution.py:555
  7.3 0.0 copy-done.3
  7.3 0.7 fusion.9
  8.0 2.6 %select_convert_fusion = f32[512]{0:T(512)S(1)} fusion(s32[]{:T(128)} %bitcast.12, s32[]{:T(128)} %bitcast.11, s32[]{:T(128)} %bitcast.10, s32[]{:T(128)} %bitcast.9), kind=kLoop, calls=%fused_computation.7 | loop fusion | flops 8192 | bytes 2064 | tf_op jit(solution)/shard_map/convert_element_type | solution.py:556
  10.7 0.6 broadcast_in_dim.40.row_expert
  11.3 0.0 copy-done.2
  11.3 0.1 concatenate.15
  11.3 0.3 copy.14
  11.6 1.0 fusion.w_pad
  12.6 0.0 copy-done
  12.6 1.2 copy.12
  13.8 0.0 copy-done.1
  13.8 1.2 copy.13
  14.9 99.4 %grad_sums.1.sums = bf16[3,192,128]{2,1,0:T(8,128)(2,1)} custom-call(bf16[512,2048]{1,0:T(8,128)(2,1)} %broadcast_select_fusion.masked, bf16[512,2048]{1,0:T(8,128)(2,1)} %tokens.1, bf16[2,384,512]{2,1,0:T(8,128)(2,1)} %bitcast.44, bf16[2,384,512]{2,1,0:T(8,128)(2,1)} %bitcast.45, f32[8,512]{1,0:T(8,128)} %broadcast_in_dim.40.row_expert, ...), custom_call_target="tpu_custom_call" | custom-call | tf_op jit(solution)/shard_map/grad_sums/pallas_call | solution.py:330
  114.3 65.5 %newton.1 = bf16[2,4,768,128]{3,2,1,0:T(8,128)(2,1)} custom-call(bf16[3,192,128]{2,1,0:T(8,128)(2,1)} %grad_sums.1.sums), custom_call_target="tpu_custom_call" | custom-call | tf_op jit(solution)/shard_map/newton/pallas_call | solution.py:513
  179.8 1.9 %constant_dynamic-slice_fusion = (bf16[1,4,768,64]{3,2,1,0:T(8,128)(2,1)S(1)}, bf16[1,4,768,64]{3,2,1,0:T(8,128)(2,1)S(1)}) fusion(bf16[2,4,768,128]{3,2,1,0:T(8,128)(2,1)} %newton.1, s32[]{:T(128)S(6)} %select_n.42, s32[]{:T(128)S(6)} %add.38), kind=kLoop, calls=%fused_computation.21 | loop fusion | bytes 1572872 | tf_op jit(solution)/shard_map/slice | solution.py:568
  181.7 0.2 copy.18
  181.9 0.3 copy.17
  182.1 0.9 pad_maximum_fusion
  (3 shorter events, 0.0 us)
Async XLA Ops:
  4.1 3.3 %copy-start.3 = (s32[4]{0:T(128)S(1)}, s32[4]{0:T(128)}, u32[]{:S(2)}) copy-start(s32[4]{0:T(128)} %param.18) | copy-start | bytes 52
  4.1 7.2 %copy-start.2 = (bf16[2,768,64]{1,2,0:T(8,128)(2,1)S(1)}, bf16[2,768,64]{1,2,0:T(8,128)(2,1)}, u32[]{:S(2)}) copy-start(bf16[2,768,64]{1,2,0:T(8,128)(2,1)} %param.17) | copy-start | bytes 589828
  4.1 8.5 %copy-start = (bf16[512,768]{1,0:T(8,128)(2,1)S(1)}, bf16[512,768]{1,0:T(8,128)(2,1)}, u32[]{:S(2)}) copy-start(bf16[512,768]{1,0:T(8,128)(2,1)} %param.15) | copy-start | bytes 2359300
  7.3 6.4 %copy-start.1 = (bf16[512,768]{1,0:T(8,128)(2,1)S(1)}, bf16[512,768]{1,0:T(8,128)(2,1)}, u32[]{:S(2)}) copy-start(bf16[512,768]{1,0:T(8,128)(2,1)} %param.16) | copy-start | bytes 2359300

commit v2 on v1

v2 whole, which is shorter than its diff:
```python
import functools

import jax
import jax.numpy as jnp
from jax import lax
from jax.experimental import pallas as pl
from jax.experimental.pallas import tpu as pltpu
from jax.sharding import Mesh
from jax.sharding import PartitionSpec as P

D = 2048
F = 768
ROWS = 512
BLOCK = 128
HALF = F // 2
THIRD = HALF // 2
LANES = 128
AXES = ("z", "x", "y")
UNITS = (
    (0, 128, ("x", "z", "y"), False),
    (128, 128, ("y", "x", "z"), False),
    (256, 64, ("z", "x", "y"), False),
    (320, 64, ("z", "y", "x"), False),
    (0, 128, ("y", "z", "x"), True),
    (128, 64, ("y", "x", "z"), True),
)
STEPS = (
    ("hid", 0, ""),
    ("wn", 0, "m"),
    ("wn", 1, "m"),
    ("pd", 0, ""),
    ("wn", 0, "f"),
    ("wn", 1, "f"),
    (4, 0, "m"),
    ("wf", 0, "m"),
    ("wf", 1, "m"),
    (5, 0, "m"),
    ("wf", 0, "f"),
    ("wf", 1, "f"),
    ("wfull", 0, ""),
    ("back", 0, ""),
    ("p0", 0, ""),
    (4, 0, "f"),
    (5, 0, "f"),
    ("p1", 0, ""),
    (4, 1, "m"),
    ("p2", 0, ""),
    ("p3", 0, ""),
    (0, 0, "m"),
    (4, 1, "f"),
    (2, 0, "m"),
    (1, 0, "m"),
    (5, 1, "m"),
    (3, 0, "m"),
    (0, 0, "f"),
    (4, 2, "m"),
    (5, 1, "f"),
    (2, 0, "f"),
    (4, 2, "f"),
    (1, 0, "f"),
    (2, 1, "m"),
    (3, 0, "f"),
    (0, 1, "m"),
    (1, 1, "m"),
    (3, 1, "m"),
    (5, 2, "m"),
    (2, 1, "f"),
    (0, 1, "f"),
    (5, 2, "f"),
    (3, 1, "f"),
    (1, 1, "f"),
    (2, 2, "m"),
    (0, 2, "m"),
    (3, 2, "m"),
    (1, 2, "m"),
    (2, 2, "f"),
    (0, 2, "f"),
    (3, 2, "f"),
    (1, 2, "f"),
)
MESH = pl.DeviceIdType.MESH

ns_first = 3.4445
ns_second = -4.775
ns_third = 2.0315
norm_eps = 1e-07

bf16 = jnp.bfloat16
f32 = jnp.float32


def around(axis):
    i = lax.axis_index(axis)
    return i, lax.rem(i + 1, 4), lax.rem(i + 3, 4), lax.rem(i + 2, 4)


def push(src, dst, send, recv, device):
    copy = pltpu.make_async_remote_copy(
        src_ref=src, dst_ref=dst, send_sem=send, recv_sem=recv, device_id=device, device_id_type=MESH
    )
    copy.start()
    return copy


def greet(axes, others):
    barrier = pltpu.get_barrier_semaphore()
    count = 0
    for axis in axes:
        i, right, left, far = around(axis)
        for other in (right, left):
            pl.semaphore_signal(barrier, inc=1, device_id={axis: other}, device_id_type=MESH)
            count += 1
    for device in others:
        pl.semaphore_signal(barrier, inc=1, device_id=device, device_id_type=MESH)
        count += 1
    pl.semaphore_wait(barrier, count)


class Scatter:
    def __init__(self, axis, src, first, second, near, final, send, recv, add):
        self.axis, self.src, self.first, self.second = axis, src, first, second
        self.near, self.final, self.send, self.recv, self.add = near, final, send, recv, add

    def start(self):
        i, right, left, far = around(self.axis)
        src, first, second, send, recv = self.src, self.first, self.second, self.send, self.recv
        to_right, to_left = {self.axis: right}, {self.axis: left}
        self.a1 = push(first(src.at[far]), first(self.near), send.at[0], recv.at[0], to_right)
        self.b1 = push(second(src.at[far]), second(self.near), send.at[1], recv.at[1], to_left)
        self.a2 = push(second(src.at[right]), second(self.final.at[0]), send.at[2], recv.at[2], to_right)
        self.b2 = push(first(src.at[left]), first(self.final.at[1]), send.at[3], recv.at[3], to_left)

    def middle(self):
        i, right, left, far = around(self.axis)
        src, first, second, send, recv = self.src, self.first, self.second, self.send, self.recv
        self.a1.wait_recv()
        self.add(first(src.at[right]), (first(self.near),))
        self.a3 = push(first(src.at[right]), first(self.final.at[0]), send.at[4], recv.at[4], {self.axis: right})
        self.b1.wait_recv()
        self.add(second(src.at[left]), (second(self.near),))
        self.b3 = push(second(src.at[left]), second(self.final.at[1]), send.at[5], recv.at[5], {self.axis: left})

    def finish(self):
        i, right, left, far = around(self.axis)
        for copy in (self.a2, self.b2, self.a3, self.b3):
            copy.wait_recv()
        self.add(self.src.at[i], (self.final.at[0], self.final.at[1]))

    def drain(self):
        for copy in (self.a1, self.b1, self.a2, self.b2, self.a3, self.b3):
            copy.wait_send()


class Gather:
    def __init__(self, axis, buf, first, second, send, recv):
        self.axis, self.buf, self.first, self.second = axis, buf, first, second
        self.send, self.recv = send, recv

    def start(self):
        i, right, left, far = around(self.axis)
        buf = self.buf
        self.a1 = push(buf.at[i], buf.at[i], self.send.at[0], self.recv.at[0], {self.axis: right})
        self.b1 = push(buf.at[i], buf.at[i], self.send.at[1], self.recv.at[1], {self.axis: left})

    def middle(self):
        i, right, left, far = around(self.axis)
        buf, first, second = self.buf, self.first, self.second
        self.a1.wait_recv()
        self.a2 = push(first(buf.at[left]), first(buf.at[left]), self.send.at[2], self.recv.at[2], {self.axis: right})
        self.b1.wait_recv()
        self.b2 = push(second(buf.at[right]), second(buf.at[right]), self.send.at[3], self.recv.at[3], {self.axis: left})

    def finish(self):
        self.a2.wait_recv()
        self.b2.wait_recv()

    def drain(self):
        for copy in (self.a1, self.b1, self.a2, self.b2):
            copy.wait_send()


def add_blocks(dst, others):
    lead = dst.shape[:-2]
    count = 1
    for size in lead:
        count *= size

    def one(n, carry):
        index = []
        rest = n
        for size in reversed(lead):
            index.append(lax.rem(rest, size))
            rest = lax.div(rest, size)
        index = tuple(reversed(index))
        total = dst[index].astype(f32)
        for other in others:
            total = total + other[index].astype(f32)
        dst[index] = total.astype(bf16)
        return carry

    if count == 1:
        one(0, 0)
    else:
        lax.fori_loop(0, count, one, 0)


def lead_halves(size):
    half = size // 2
    return (lambda ref: ref.at[pl.ds(0, half)]), (lambda ref: ref.at[pl.ds(half, half)])


NT = (((1,), (1,)), ((), ()))


def grad_kernel(
    experts, counts, cotangent, tokens, gate, up, weight_t, out,
    mk, tk, gb, ub, gt, ut, rex, wx, wall, wfull, back_ref, left_g, left_d, *rest
):
    own_sem, x_send, x_recv, w_send, w_recv, r_send, r_recv = rest[-7:]
    buffers = [rest[7 * k:7 * k + 7] for k in range(len(UNITS))]
    c = lax.axis_index("core")
    other = {"core": 1 - c}
    mine = pl.ds(pl.multiple_of(c * HALF, HALF), HALF)
    theirs = pl.ds(pl.multiple_of((1 - c) * HALF, HALF), HALF)
    own = []
    for n, (src, dst) in enumerate((
        (weight_t.at[:, :, mine], wx.at[c]),
        (gate.at[:, mine], gb.at[0]),
        (up.at[:, mine], ub.at[0]),
        (cotangent, mk.at[0]),
        (tokens, tk.at[0]),
    )):
        copy = pltpu.make_async_copy(src, dst, own_sem.at[n])
        copy.start()
        own.append(copy)
    lane = lax.broadcasted_iota(jnp.int32, (8, BLOCK), 1)
    for b in range(ROWS // BLOCK):
        code = jnp.where(lane < counts[b], experts[b], 2)
        rex[0, :, b * BLOCK:(b + 1) * BLOCK] = code.astype(f32)
    greet(AXES, (other,))
    cross = []
    for n, (src, dst) in enumerate((
        (weight_t.at[:, :, theirs], wx.at[c]),
        (gate.at[:, theirs], gb.at[1]),
        (up.at[:, theirs], ub.at[1]),
        (cotangent, mk.at[1]),
        (tokens, tk.at[1]),
        (rex.at[0], rex.at[1]),
    )):
        cross.append(push(src, dst, x_send.at[n], x_recv.at[n], other))

    def ready(n):
        if n < 5:
            own[n].wait()
        cross[n].wait_recv()

    z, x = lax.axis_index("z"), lax.axis_index("x")
    first, second = lead_halves(HALF)
    four_first, four_second = lead_halves(4)
    w_near = [
        Gather("z", wall.at[0, x], first, second, w_send.at[0], w_recv.at[0]),
        Gather("x", wall.at[1, z], first, second, w_send.at[1], w_recv.at[1]),
    ]
    w_far = [
        Gather("x", wall.at[0], four_first, four_second, w_send.at[2], w_recv.at[2]),
        Gather("z", wall.at[1], four_first, four_second, w_send.at[3], w_recv.at[3]),
    ]
    ready(0)
    for e in range(2):
        block = jnp.concatenate([wx[0, e], wx[1, e]], axis=0).astype(f32).T.astype(bf16)
        if e == 0:
            wall[0, x, z] = block
        else:
            wall[1, z, x] = block
    for one in w_near:
        one.start()

    rs = []
    cut = lead_halves(4)
    for k, (start, rows, order, down) in enumerate(UNITS):
        a, b = lax.axis_index(order[0]), lax.axis_index(order[1])
        part, near0, fin0, near1, fin1, near2, fin2 = buffers[k]
        rs.append(
            (
                Scatter(order[0], part, *cut, near0, fin0, r_send.at[k, 0], r_recv.at[k, 0], add_blocks),
                Scatter(order[1], part.at[a], *cut, near1, fin1, r_send.at[k, 1], r_recv.at[k, 1], add_blocks),
                Scatter(order[2], part.at[a, b], *lead_halves(rows), near2, fin2, r_send.at[k, 2], r_recv.at[k, 2], add_blocks),
            )
        )

    def make_hidden():
        for n in (1, 2, 5):
            ready(n)
        for s in range(2):
            @pl.loop(0, ROWS // BLOCK)
            def hidden_rows(t, s=s):
                rows = pl.ds(pl.multiple_of(t * BLOCK, BLOCK), BLOCK)
                there = pl.ds(pl.multiple_of(s * ROWS + t * BLOCK, BLOCK), BLOCK)
                g = gb[s, rows, :].astype(f32).T
                u = ub[s, rows, :].astype(f32).T
                gt[s, :, rows] = g.astype(bf16)
                ut[s, :, rows] = u.astype(bf16)
                hidden = g * jax.nn.sigmoid(g) * u
                which = rex[s, 0:1, rows]
                for e in range(2):
                    kept = jnp.where(which == e, hidden, 0.0).astype(bf16)
                    for h in range(2):
                        left_d[2 * e + h, :, there] = kept[h * THIRD:(h + 1) * THIRD]

    def products(picked):
        down = UNITS[picked[0]][3]
        lhs_ref, right = (left_d, mk) if down else (left_g, tk)
        low = UNITS[picked[0]][0]
        size = sum(UNITS[k][1] for k in picked)

        @pl.loop(0, 4)
        def columns(iz):
            cols = pl.ds(pl.multiple_of(iz * 512, 512), 512)
            lhs = lhs_ref[:, low:low + size, :].reshape(4 * size, 2 * ROWS)
            rhs = right[:, :, cols].reshape(2 * ROWS, 512)
            acc = jnp.dot(lhs, rhs, preferred_element_type=f32).astype(bf16)
            for k in picked:
                start, rows, order, _ = UNITS[k]
                for y in range(4):
                    first = y * size + start - low
                    for ix in range(4):
                        where = {"z": iz, "x": ix, "y": y}
                        index = tuple(where[axis] for axis in order)
                        buffers[k][0][index] = acc[first:first + rows, ix * LANES:(ix + 1) * LANES]

        for k in picked:
            rs[k][0].start()

    def pack_weights():
        for iz in range(4):
            for ix in range(4):
                cols = slice((iz * 4 + ix) * LANES, (iz * 4 + ix + 1) * LANES)
                wfull[0:HALF, cols] = wall[0, ix, iz]
                wfull[HALF:, cols] = wall[1, iz, ix]

    def make_back():
        tile = 32
        for s in range(2):
            @pl.loop(0, 2)
            def back_columns(t, s=s):
                rows = pl.ds(pl.multiple_of(t * 256, 256), 256)
                back_ref[:, rows] = lax.dot_general(wfull[...], mk[s, rows, :], NT, preferred_element_type=f32)

            @pl.loop(0, HALF // tile)
            def back_rows(t, s=s):
                rows = pl.ds(pl.multiple_of(t * tile, tile), tile)
                low = pl.ds(pl.multiple_of(HALF + t * tile, tile), tile)
                which = rex[s, 0:1, :]
                back = jnp.where(which == 0, back_ref[rows, :], back_ref[low, :])
                g = gt[s, rows, :].astype(f32)
                u = ut[s, rows, :].astype(f32)
                sig = jax.nn.sigmoid(g)
                grads = (back * u * sig * (1.0 + g * (1.0 - sig)), back * g * sig)
                for e in range(2):
                    for h in range(2):
                        kept = jnp.where(which == e, grads[h], 0.0).astype(bf16)
                        left_g[2 * e + h, rows, s * ROWS:(s + 1) * ROWS] = kept

    def advance(unit, phase, what):
        if what == "m":
            rs[unit][phase].middle()
        else:
            rs[unit][phase].finish()
            if phase < 2:
                rs[unit][phase + 1].start()

    for name, e, what in STEPS:
        if name == "hid":
            make_hidden()
        elif name == "pd":
            ready(3)
            products([k for k in range(len(UNITS)) if UNITS[k][3]])
        elif name == "wfull":
            pack_weights()
        elif name == "back":
            make_back()
            ready(4)
        elif name == "wn":
            if what == "m":
                w_near[e].middle()
            else:
                w_near[e].finish()
                w_far[e].start()
        elif name == "wf":
            if what == "m":
                w_far[e].middle()
            else:
                w_far[e].finish()
        elif isinstance(name, str):
            products([int(name[1:])])
        else:
            advance(name, e, what)
    for k, (start, rows, order, down) in enumerate(UNITS):
        a, b, d = (lax.axis_index(axis) for axis in order)
        start = start + (HALF if down else 0)
        out[start:start + rows, :] = buffers[k][0][a, b, d]
    for copy in cross:
        copy.wait_send()
    for one in w_near + w_far:
        one.drain()
    for unit in rs:
        for one in unit:
            one.drain()


def grad_sums(experts, counts, cotangent, tokens, gate, up, weight_t):
    anywhere = pl.BlockSpec(memory_space=pl.ANY)
    smem = pl.BlockSpec(memory_space=pltpu.SMEM)
    vmem = pltpu.VMEM
    dma = pltpu.SemaphoreType.DMA
    buffers = []
    for start, rows, order, down in UNITS:
        block = (rows, LANES)
        for lead in ((4, 4, 4), (4, 4), (2, 4, 4), (4,), (2, 4), (), (2,)):
            buffers.append(vmem(lead + block, bf16))
    return pl.pallas_call(
        grad_kernel,
        out_shape=jax.ShapeDtypeStruct((3 * THIRD, LANES), bf16),
        in_specs=[smem] * 2 + [anywhere] * 5,
        out_specs=pl.BlockSpec(memory_space=vmem),
        scratch_shapes=[
            vmem((2, ROWS, D), bf16),
            vmem((2, ROWS, D), bf16),
            vmem((2, ROWS, HALF), bf16),
            vmem((2, ROWS, HALF), bf16),
            vmem((2, HALF, ROWS), bf16),
            vmem((2, HALF, ROWS), bf16),
            vmem((2, 8, ROWS), f32),
            vmem((2, 2, LANES // 2, HALF), bf16),
            vmem((2, 4, 4, HALF, LANES), bf16),
            vmem((F, D), bf16),
            vmem((F, ROWS), f32),
            vmem((4, HALF, 2 * ROWS), bf16),
            vmem((4, THIRD, 2 * ROWS), bf16),
            *buffers,
            dma((5,)),
            dma((6,)),
            dma((6,)),
            dma((4, 4)),
            dma((4, 4)),
            dma((len(UNITS), 3, 6)),
            dma((len(UNITS), 3, 6)),
        ],
        compiler_params=pltpu.CompilerParams(
            collective_id=0, has_side_effects=True, vmem_limit_bytes=62 * 1024 * 1024
        ),
        name="grad_sums",
    )(experts, counts, cotangent, tokens, gate, up, weight_t)


CHUNK = 96
PAIRS = ((0, 0), (0, 1), (0, 2), (1, 1), (1, 2), (2, 2))
WIDE = 256
STRIP = 32


def strips():
    for n in range(len(PAIRS) * WIDE // STRIP):
        row = n * STRIP
        yield n // 8, (n % 8) * STRIP, row // CHUNK, row % CHUNK


def newton_kernel(
    sums, out,
    pair, from_core, pair_core, mat, gram, whole, near0, fin0, near1, fin1,
    g1, p1, u, g2, p2, ring0, ring1,
    x_send, x_recv, g_send, g_recv, a_send, a_recv, o_send, o_recv,
):
    c, y = lax.axis_index("core"), lax.axis_index("y")
    h = lax.rem(y, 2)
    mate = y + 1 - 2 * h
    other = {"core": 1 - c}
    greet(AXES, (other, {"y": mate, "core": 1 - c}))
    low_rows = sums.at[pl.ds(HALF, THIRD)]
    down = push(low_rows, pair, x_send.at[0], x_recv.at[0], {"y": mate})
    onward = push(low_rows, pair_core, x_send.at[2], x_recv.at[2], {"y": mate, "core": 1 - c})
    swap = push(sums, from_core, x_send.at[1], x_recv.at[1], other)
    for copy in (swap, down, onward):
        copy.wait_recv()

    @pl.when(c == 0)
    def first_core():
        for k in range(2):
            mat[k] = sums[k * THIRD:(k + 1) * THIRD]
            mat[2 + k] = from_core[k * THIRD:(k + 1) * THIRD]

    @pl.when(c == 1)
    def second_core():
        mat[h] = from_core[HALF:]
        mat[1 - h] = pair_core[...]
        mat[2 + h] = sums[HALF:]
        mat[3 - h] = pair[...]

    X = mat[...].reshape(F, LANES)
    blocks = []
    for i, j in PAIRS:
        left, right = X[i * WIDE:(i + 1) * WIDE], X[j * WIDE:(j + 1) * WIDE]
        blocks.append(lax.dot_general(left, right, NT, preferred_element_type=f32).astype(bf16))
    for n, rows, chunk, place in strips():
        for k in range(2):
            gram[k, chunk // 4, chunk % 4, place:place + STRIP, :] = blocks[n][
                rows:rows + STRIP, k * LANES:(k + 1) * LANES
            ]

    four = lead_halves(4)
    halves = lead_halves(CHUNK)
    orders = (("z", "x"), ("x", "z"))
    rs0, rs1, ag0, ag1 = [], [], [], []
    for k in range(2):
        first_axis, second_axis = orders[k]
        a = lax.axis_index(first_axis)
        rs0.append(Scatter(first_axis, gram.at[k], *four, near0.at[k], fin0.at[k], g_send.at[k, 0], g_recv.at[k, 0], add_blocks))
        rs1.append(Scatter(second_axis, gram.at[k, a], *halves, near1.at[k], fin1.at[k], g_send.at[k, 1], g_recv.at[k, 1], add_blocks))
        ag0.append(Gather(second_axis, whole.at[k, a], *halves, a_send.at[k, 0], a_recv.at[k, 0]))
        ag1.append(Gather(first_axis, whole.at[k], *four, a_send.at[k, 1], a_recv.at[k, 1]))
    for k in range(2):
        rs0[k].start()
    for k in range(2):
        rs0[k].middle()
    for k in range(2):
        rs0[k].finish()
        rs1[k].start()
    for k in range(2):
        rs1[k].middle()
    for k in range(2):
        rs1[k].finish()
        a, b = (lax.axis_index(axis) for axis in orders[k])
        whole[k, a, b] = gram[k, a, b]
        ag0[k].start()
    for k in range(2):
        ag0[k].middle()
    for k in range(2):
        ag0[k].finish()
        ag1[k].start()
    for k in range(2):
        ag1[k].middle()
    for k in range(2):
        ag1[k].finish()

    trace = jnp.zeros((STRIP, LANES), f32)
    row = lax.broadcasted_iota(jnp.int32, (STRIP, LANES), 0)
    col = lax.broadcasted_iota(jnp.int32, (STRIP, LANES), 1)
    for n, rows, chunk, place in strips():
        if PAIRS[n][0] == PAIRS[n][1]:
            k = rows // LANES
            value = whole[k, chunk // 4, chunk % 4, place:place + STRIP, :].astype(f32)
            trace = trace + jnp.where(col == row + rows % LANES, value, 0.0)
    squares = jnp.sum(jnp.sum(trace, axis=0, keepdims=True), axis=1, keepdims=True)
    scale = 1.0 / (jnp.sqrt(squares) + norm_eps)
    for n, rows, chunk, place in strips():
        i, j = PAIRS[n]
        for k in range(2):
            value = whole[k, chunk // 4, chunk % 4, place:place + STRIP, :].astype(f32) * scale * scale
            g1[i * WIDE + rows:i * WIDE + rows + STRIP, j * WIDE + k * LANES:j * WIDE + (k + 1) * LANES] = value.astype(bf16)
    for i, j in PAIRS:
        if i != j:
            block = g1[i * WIDE:(i + 1) * WIDE, j * WIDE:(j + 1) * WIDE]
            g1[j * WIDE:(j + 1) * WIDE, i * WIDE:(i + 1) * WIDE] = block.astype(f32).T.astype(bf16)

    def times(left, right, cols):
        return jnp.dot(left[...], right[:, cols], preferred_element_type=f32)

    def make_p1(cols):
        p1[:, cols] = (ns_second * g1[:, cols].astype(f32) + ns_third * times(g1, g1, cols)).astype(bf16)

    def make_u(cols):
        u[:, cols] = (ns_first * g1[:, cols].astype(f32) + times(p1, g1, cols)).astype(bf16)

    def make_g2(cols):
        g2[:, cols] = (ns_first * u[:, cols].astype(f32) + times(p1, u, cols)).astype(bf16)

    def make_p2(cols):
        p2[:, cols] = (ns_second * g2[:, cols].astype(f32) + ns_third * times(g2, g2, cols)).astype(bf16)

    def make_rest(cols):
        rest = ns_first * (p1[:, cols].astype(f32) + p2[:, cols].astype(f32)) + times(p2, p1, cols)
        u[:, cols] = rest.astype(bf16)

    for body in (make_p1, make_u, make_g2, make_p2, make_rest):
        @pl.loop(0, F // WIDE)
        def one(t, body=body):
            body(pl.ds(pl.multiple_of(t * WIDE, WIDE), WIDE))

    factor = scale * jnp.sqrt(f32(D))
    XT = X.astype(f32).T
    low = XT.astype(bf16)
    i, right, left, far = around("y")
    side = LANES // 2

    @pl.when(c == 0)
    def send_first():
        new = ns_first * ns_first * XT + jnp.dot(low, u[...], preferred_element_type=f32)
        ring0[i] = (factor * new).astype(bf16)
        ring = Gather("y", ring0, *lead_halves(LANES), o_send.at[0], o_recv.at[0])
        place = lambda t: out.at[lax.div(t, 2), lax.rem(t, 2)]
        give = lambda t, n: push(ring0.at[t, pl.ds(side, side)], place(t), x_send.at[n], x_recv.at[n], other)
        ring.start()
        over = [give(i, 3)]
        ring.middle()
        over.append(give(left, 4))
        over.append(give(right, 5))
        ring.finish()
        over.append(give(far, 6))
        for t in range(4):
            out[t // 2, t % 2] = ring0[t, 0:side]
        for n, t in enumerate((i, left, right, far)):
            span = pl.ds(pl.multiple_of(lax.rem(t, 2) * HALF, HALF), HALF)
            expected = out.at[lax.div(t, 2), 2, :, span]
            pltpu.make_async_remote_copy(
                src_ref=expected, dst_ref=expected, send_sem=x_send.at[3 + n], recv_sem=x_recv.at[3 + n],
                device_id=other, device_id_type=MESH,
            ).wait_recv()
        for copy in over:
            copy.wait_send()
        ring.drain()

    @pl.when(c == 1)
    def send_second():
        half = pl.ds(pl.multiple_of(h * HALF, HALF), HALF)
        g2[0:LANES, 0:HALF] = jnp.where(h == 0, XT[:, 0:HALF], XT[:, HALF:]).astype(bf16)
        new = ns_first * ns_first * g2[0:LANES, 0:HALF].astype(f32) + jnp.dot(
            low, u[:, half], preferred_element_type=f32
        )
        ring1[i] = (factor * new).astype(bf16)
        ring = Gather("y", ring1, *lead_halves(LANES), o_send.at[1], o_recv.at[1])
        place = lambda t: out.at[lax.div(t, 2), 2, :, pl.ds(pl.multiple_of(lax.rem(t, 2) * HALF, HALF), HALF)]
        give = lambda t, n: push(ring1.at[t, pl.ds(0, side)], place(t), x_send.at[n], x_recv.at[n], other)
        ring.start()
        over = [give(i, 3)]
        ring.middle()
        over.append(give(left, 4))
        over.append(give(right, 5))
        ring.finish()
        over.append(give(far, 6))
        for t in range(4):
            out[t // 2, 2, :, (t % 2) * HALF:(t % 2 + 1) * HALF] = ring1[t, side:]
        for n, t in enumerate((i, left, right, far)):
            expected = out.at[lax.div(t, 2), lax.rem(t, 2)]
            pltpu.make_async_remote_copy(
                src_ref=expected, dst_ref=expected, send_sem=x_send.at[3 + n], recv_sem=x_recv.at[3 + n],
                device_id=other, device_id_type=MESH,
            ).wait_recv()
        for copy in over:
            copy.wait_send()
        ring.drain()

    for copy in (down, swap, onward):
        copy.wait_send()
    for one in rs0 + rs1 + ag0 + ag1:
        one.drain()


def newton(sums):
    vmem = pltpu.VMEM
    dma = pltpu.SemaphoreType.DMA
    square = vmem((F, F), bf16)
    return pl.pallas_call(
        newton_kernel,
        out_shape=jax.ShapeDtypeStruct((2, 3, LANES // 2, F), bf16),
        in_specs=[pl.BlockSpec(memory_space=vmem)],
        out_specs=pl.BlockSpec(memory_space=vmem),
        scratch_shapes=[
            vmem((THIRD, LANES), bf16),
            vmem((3 * THIRD, LANES), bf16),
            vmem((THIRD, LANES), bf16),
            vmem((4, THIRD, LANES), bf16),
            vmem((2, 4, 4, CHUNK, LANES), bf16),
            vmem((2, 4, 4, CHUNK, LANES), bf16),
            vmem((2, 4, CHUNK, LANES), bf16),
            vmem((2, 2, 4, CHUNK, LANES), bf16),
            vmem((2, CHUNK, LANES), bf16),
            vmem((2, 2, CHUNK, LANES), bf16),
            square, square, square, square, square,
            vmem((4, LANES, F), bf16),
            vmem((4, LANES, HALF), bf16),
            dma((7,)),
            dma((7,)),
            dma((2, 2, 6)),
            dma((2, 2, 6)),
            dma((2, 2, 4)),
            dma((2, 2, 4)),
            dma((2, 4)),
            dma((2, 4)),
        ],
        compiler_params=pltpu.CompilerParams(
            collective_id=1, has_side_effects=True, vmem_limit_bytes=60 * 1024 * 1024
        ),
        name="newton",
    )(sums)


def per_device(
    token_inputs, cotangent, gate_preact, up_preact, down_weight, block_expert, block_count
):
    sums = grad_sums(
        block_expert, block_count, cotangent, token_inputs, gate_preact, up_preact,
        down_weight.swapaxes(1, 2),
    )
    return newton(sums).swapaxes(2, 3)


def solution(mesh):
    torus = Mesh(mesh.devices.reshape(4, 4, 2, mesh.shape["rep"]), ("z", "x", "core", "y"))
    dp, dp_rep = ("z", "x", "core"), ("z", "x", "core", "y")
    return jax.shard_map(
        per_device,
        mesh=torus,
        in_specs=(
            P(dp_rep, None),
            P(dp_rep, None),
            P(dp_rep, None),
            P(dp_rep, None),
            P(None, None, dp),
            P(dp_rep),
            P(dp_rep),
        ),
        out_specs=P(None, None, None, dp),
        check_vma=False,
    )
```

time: 183 us -> 151 us (0.83)
  Pallas kernels: 165 us -> 149 us
  other arithmetic: 10.3 us -> 0 us
  local copies, waits for them, and re-layouts: 7.74 us -> 1.92 us
    pallas_call x2, Pallas kernels: 165 us -> 149 us  [the longest x1 87.2 us: grad_sums(): pl.pallas_call(grad_kernel, out_shape=jax.ShapeDtypeStruct((3 * THIRD, LA...]
    select_n x1 -> x0, other arithmetic: 3.24 us -> none  [per_device(): jnp.where((row_place < row_count)[:, None], cotangent, jnp.zeros_like(cot...]
    convert_element_type x1 -> x0, other arithmetic: 2.64 us -> none  [per_device(): jnp.repeat(block_expert, block_rows, total_repeat_length=rows_here)]
    lt x1 -> x0, other arithmetic: 2.58 us -> none  [per_device(): row_place < row_count]
    transpose x2 -> x0, local copies, waits for them, and re-layouts: 2.33 us -> none  [the longest x1 1.17 us: per_device(): up_t = up_preact.T.reshape(2, HALF, rows_here)]
    gather x2 -> x0, local copies, waits for them, and re-layouts: 2.13 us -> none  [the longest x1 1.47 us: per_device(): jnp.repeat(block_count, block_rows, total_repeat_length=rows_here)]
    slice x2 -> x0, local copies, waits for them, and re-layouts: 1.89 us -> none  [the longest x1 1.87 us: per_device(): top = mine[0].reshape(2, 2, F, cols)]
where the time goes in v2:
time: 151 us
  Pallas kernels  149 us (99%)
  local copies, waits for them, and re-layouts  1.92 us (1%)
    pallas_call x1, Pallas kernels, grad_sums(): pl.pallas_call(grad_kernel, out_shape=jax.ShapeDtypeStruct((3 * THIRD, LA...  87.2 us
    pallas_call x1, Pallas kernels, newton(): pl.pallas_call(newton_kernel, out_shape=jax.ShapeDtypeStruct((2, 3, LANES...  62.1 us

profile of v2, /device:TPU:1, one launch (start us, length us, event | category | flops | bytes accessed | tf_op | source)
XLA Modules:
  0.0 151.3 jit_solution(8932362763699118516)
XLA Ops:
  0.0 87.2 %grad_sums.1.sums = bf16[576,128]{1,0:T(8,128)(2,1)} custom-call(s32[4]{0:T(128)} %experts.1, s32[4]{0:T(128)} %counts.1, bf16[512,2048]{1,0:T(8,128)(2,1)} %cotangent.1, bf16[512,2048]{1,0:T(8,128)(2,1)} %tokens.1, bf16[512,768]{1,0:T(8,128)(2,1)} %gate.1, bf16[512,768]{1,0:T(8,128)(2,1)} %up.1, bf16[2,64,768]{2,1,0:T(8,128)(2,1)} %bitcast.3), custom_call_target="tpu_custom_call" | custom-call | tf_op jit(solution)/shard_map/grad_sums/pallas_call | solution.py:421
  87.3 62.1 %newton.1 = bf16[2,3,64,768]{3,2,1,0:T(8,128)(2,1)} custom-call(bf16[576,128]{1,0:T(8,128)(2,1)} %grad_sums.1.sums), custom_call_target="tpu_custom_call" | custom-call | tf_op jit(solution)/shard_map/newton/pallas_call | solution.py:662
  149.3 1.9 %copy.9 = bf16[2,3,768,64]{2,3,1,0:T(8,128)(2,1)} copy(bf16[2,3,768,64]{2,3,1,0:T(8,128)(2,1)} %bitcast.2) | data formatting | bytes 1179648

commit v3 on v2

--- a/solution.py
+++ b/solution.py
@@ -17,66 +17,78 @@
 LANES = 128
 AXES = ("z", "x", "y")
 UNITS = (
-    (0, 128, ("x", "z", "y"), False),
-    (128, 128, ("y", "x", "z"), False),
-    (256, 64, ("z", "x", "y"), False),
-    (320, 64, ("z", "y", "x"), False),
-    (0, 128, ("y", "z", "x"), True),
-    (128, 64, ("y", "x", "z"), True),
+    (0, 64, ("x", "y", "z"), False),
+    (64, 64, ("y", "z", "x"), False),
+    (128, 64, ("z", "y", "x"), False),
+    (192, 64, ("y", "x", "z"), False),
+    (256, 64, ("z", "y", "x"), False),
+    (320, 64, ("x", "z", "y"), False),
+    (0, 192, ("y", "x", "z"), True),
 )
 STEPS = (
     ("hid", 0, ""),
+    ("pd", 0, ""),
     ("wn", 0, "m"),
     ("wn", 1, "m"),
-    ("pd", 0, ""),
     ("wn", 0, "f"),
     ("wn", 1, "f"),
-    (4, 0, "m"),
+    (6, 0, "m"),
     ("wf", 0, "m"),
     ("wf", 1, "m"),
-    (5, 0, "m"),
     ("wf", 0, "f"),
     ("wf", 1, "f"),
     ("wfull", 0, ""),
     ("back", 0, ""),
-    ("p0", 0, ""),
+    ("prod", 0, ""),
+    ("prod", 1, ""),
+    ("back", 128, ""),
+    ("prod", 2, ""),
+    (0, 0, "m"),
+    (6, 0, "f"),
+    ("prod", 3, ""),
+    (1, 0, "m"),
+    ("back", 256, ""),
+    (2, 0, "m"),
+    (0, 0, "f"),
+    ("prod", 4, ""),
+    (3, 0, "m"),
+    (6, 1, "m"),
+    ("prod", 5, ""),
+    (2, 0, "f"),
+    (6, 1, "f"),
+    (1, 0, "f"),
+    (4, 0, "m"),
+    (0, 1, "m"),
+    (5, 0, "m"),
+    (6, 2, "m"),
+    (3, 0, "f"),
+    (1, 1, "m"),
+    (2, 1, "m"),
+    (0, 1, "f"),
+    (2, 1, "f"),
+    (5, 0, "f"),
     (4, 0, "f"),
-    (5, 0, "f"),
-    ("p1", 0, ""),
+    (3, 1, "m"),
+    (6, 2, "f"),
+    ("low", 0, ""),
+    (2, 2, "m"),
+    (1, 1, "f"),
+    (0, 2, "m"),
+    (5, 1, "m"),
     (4, 1, "m"),
-    ("p2", 0, ""),
-    ("p3", 0, ""),
-    (0, 0, "m"),
-    (4, 1, "f"),
-    (2, 0, "m"),
-    (1, 0, "m"),
-    (5, 1, "m"),
-    (3, 0, "m"),
-    (0, 0, "f"),
-    (4, 2, "m"),
-    (5, 1, "f"),
-    (2, 0, "f"),
-    (4, 2, "f"),
-    (1, 0, "f"),
-    (2, 1, "m"),
-    (3, 0, "f"),
-    (0, 1, "m"),
-    (1, 1, "m"),
-    (3, 1, "m"),
-    (5, 2, "m"),
-    (2, 1, "f"),
-    (0, 1, "f"),
-    (5, 2, "f"),
     (3, 1, "f"),
-    (1, 1, "f"),
-    (2, 2, "m"),
-    (0, 2, "m"),
-    (3, 2, "m"),
-    (1, 2, "m"),
     (2, 2, "f"),
     (0, 2, "f"),
+    (1, 2, "m"),
+    (5, 1, "f"),
+    (3, 2, "m"),
+    (4, 1, "f"),
+    (1, 2, "f"),
+    (5, 2, "m"),
     (3, 2, "f"),
-    (1, 2, "f"),
+    (4, 2, "m"),
+    (5, 2, "f"),
+    (4, 2, "f"),
 )
 MESH = pl.DeviceIdType.MESH
 
@@ -216,7 +228,13 @@
     experts, counts, cotangent, tokens, gate, up, weight_t, out,
     mk, tk, gb, ub, gt, ut, rex, wx, wall, wfull, back_ref, left_g, left_d, *rest
 ):
-    own_sem, x_send, x_recv, w_send, w_recv, r_send, r_recv = rest[-7:]
+    count = 7 * len(UNITS)
+    own_sem, x_send, x_recv, w_send, w_recv, r_send, r_recv, sums, *news = rest[count:]
+    pair, from_core, pair_core = news[:3]
+    n_send, n_recv = news[16:18]
+    y = lax.axis_index("y")
+    h = lax.rem(y, 2)
+    mate = y + 1 - 2 * h
     buffers = [rest[7 * k:7 * k + 7] for k in range(len(UNITS))]
     c = lax.axis_index("core")
     other = {"core": 1 - c}
@@ -237,7 +255,7 @@
     for b in range(ROWS // BLOCK):
         code = jnp.where(lane < counts[b], experts[b], 2)
         rex[0, :, b * BLOCK:(b + 1) * BLOCK] = code.astype(f32)
-    greet(AXES, (other,))
+    greet(AXES, (other, {"y": mate, "core": 1 - c}))
     cross = []
     for n, (src, dst) in enumerate((
         (weight_t.at[:, :, theirs], wx.at[c]),
@@ -335,23 +353,25 @@
         for iz in range(4):
             for ix in range(4):
                 cols = slice((iz * 4 + ix) * LANES, (iz * 4 + ix + 1) * LANES)
-                wfull[0:HALF, cols] = wall[0, ix, iz]
-                wfull[HALF:, cols] = wall[1, iz, ix]
-
-    def make_back():
+                wfull[0, :, cols] = wall[0, ix, iz]
+                wfull[1, :, cols] = wall[1, iz, ix]
+
+    def make_back(low):
         tile = 32
         for s in range(2):
             @pl.loop(0, 2)
             def back_columns(t, s=s):
                 rows = pl.ds(pl.multiple_of(t * 256, 256), 256)
-                back_ref[:, rows] = lax.dot_general(wfull[...], mk[s, rows, :], NT, preferred_element_type=f32)
-
-            @pl.loop(0, HALF // tile)
+                lhs = wfull[:, low:low + LANES, :].reshape(2 * LANES, D)
+                back_ref[:, rows] = lax.dot_general(lhs, mk[s, rows, :], NT, preferred_element_type=f32)
+
+            @pl.loop(0, LANES // tile)
             def back_rows(t, s=s):
-                rows = pl.ds(pl.multiple_of(t * tile, tile), tile)
-                low = pl.ds(pl.multiple_of(HALF + t * tile, tile), tile)
+                rows = pl.ds(pl.multiple_of(low + t * tile, tile), tile)
+                near = pl.ds(pl.multiple_of(t * tile, tile), tile)
+                far = pl.ds(pl.multiple_of(LANES + t * tile, tile), tile)
                 which = rex[s, 0:1, :]
-                back = jnp.where(which == 0, back_ref[rows, :], back_ref[low, :])
+                back = jnp.where(which == 0, back_ref[near, :], back_ref[far, :])
                 g = gt[s, rows, :].astype(f32)
                 u = ut[s, rows, :].astype(f32)
                 sig = jax.nn.sigmoid(g)
@@ -369,6 +389,14 @@
             if phase < 2:
                 rs[unit][phase + 1].start()
 
+    def settle(which):
+        for k, (start, rows, order, down) in enumerate(UNITS):
+            if down == which:
+                a, b, d = (lax.axis_index(axis) for axis in order)
+                start = start + (HALF if down else 0)
+                sums[start:start + rows, :] = buffers[k][0][a, b, d]
+
+    swaps = []
     for name, e, what in STEPS:
         if name == "hid":
             make_hidden()
@@ -378,8 +406,7 @@
         elif name == "wfull":
             pack_weights()
         elif name == "back":
-            make_back()
-            ready(4)
+            make_back(e)
         elif name == "wn":
             if what == "m":
                 w_near[e].middle()
@@ -391,14 +418,24 @@
                 w_far[e].middle()
             else:
                 w_far[e].finish()
-        elif isinstance(name, str):
-            products([int(name[1:])])
+        elif name == "prod":
+            if e == 0:
+                ready(4)
+            products([e])
+        elif name == "low":
+            settle(True)
+            low_rows = sums.at[pl.ds(HALF, THIRD)]
+            swaps = [
+                push(low_rows, pair, n_send.at[0], n_recv.at[0], {"y": mate}),
+                push(low_rows, pair_core, n_send.at[2], n_recv.at[2], {"y": mate, "core": 1 - c}),
+                push(low_rows, from_core.at[pl.ds(HALF, THIRD)], n_send.at[7], n_recv.at[7], other),
+            ]
         else:
             advance(name, e, what)
-    for k, (start, rows, order, down) in enumerate(UNITS):
-        a, b, d = (lax.axis_index(axis) for axis in order)
-        start = start + (HALF if down else 0)
-        out[start:start + rows, :] = buffers[k][0][a, b, d]
+    settle(False)
+    high = pl.ds(0, HALF)
+    swaps.append(push(sums.at[high], from_core.at[high], n_send.at[1], n_recv.at[1], other))
+    newton_steps(swaps, c, y, h, other, out, sums, *news)
     for copy in cross:
         copy.wait_send()
     for one in w_near + w_far:
@@ -408,11 +445,12 @@
             one.drain()
 
 
-def grad_sums(experts, counts, cotangent, tokens, gate, up, weight_t):
+def grad_update(experts, counts, cotangent, tokens, gate, up, weight_t):
     anywhere = pl.BlockSpec(memory_space=pl.ANY)
     smem = pl.BlockSpec(memory_space=pltpu.SMEM)
     vmem = pltpu.VMEM
     dma = pltpu.SemaphoreType.DMA
+    square = vmem((F, F), bf16)
     buffers = []
     for start, rows, order, down in UNITS:
         block = (rows, LANES)
@@ -420,7 +458,7 @@
             buffers.append(vmem(lead + block, bf16))
     return pl.pallas_call(
         grad_kernel,
-        out_shape=jax.ShapeDtypeStruct((3 * THIRD, LANES), bf16),
+        out_shape=jax.ShapeDtypeStruct((2, 3, LANES // 2, F), bf16),
         in_specs=[smem] * 2 + [anywhere] * 5,
         out_specs=pl.BlockSpec(memory_space=vmem),
         scratch_shapes=[
@@ -433,8 +471,8 @@
             vmem((2, 8, ROWS), f32),
             vmem((2, 2, LANES // 2, HALF), bf16),
             vmem((2, 4, 4, HALF, LANES), bf16),
-            vmem((F, D), bf16),
-            vmem((F, ROWS), f32),
+            vmem((2, HALF, D), bf16),
+            vmem((2 * LANES, ROWS), f32),
             vmem((4, HALF, 2 * ROWS), bf16),
             vmem((4, THIRD, 2 * ROWS), bf16),
             *buffers,
@@ -445,11 +483,32 @@
             dma((4, 4)),
             dma((len(UNITS), 3, 6)),
             dma((len(UNITS), 3, 6)),
+            vmem((3 * THIRD, LANES), bf16),
+            vmem((THIRD, LANES), bf16),
+            vmem((3 * THIRD, LANES), bf16),
+            vmem((THIRD, LANES), bf16),
+            vmem((4, THIRD, LANES), bf16),
+            vmem((2, 4, 4, CHUNK, LANES), bf16),
+            vmem((2, 4, 4, CHUNK, LANES), bf16),
+            vmem((2, 4, CHUNK, LANES), bf16),
+            vmem((2, 2, 4, CHUNK, LANES), bf16),
+            vmem((2, 4, 4, CHUNK, LANES), bf16),
+            square, square, square, square, square,
+            vmem((4, LANES, F), bf16),
+            vmem((4, LANES, HALF), bf16),
+            dma((8,)),
+            dma((8,)),
+            dma((2, 2, 6)),
+            dma((2, 2, 6)),
+            dma((2, 2, 4)),
+            dma((2, 2, 4)),
+            dma((2, 4)),
+            dma((2, 4)),
         ],
         compiler_params=pltpu.CompilerParams(
-            collective_id=0, has_side_effects=True, vmem_limit_bytes=62 * 1024 * 1024
+            collective_id=0, has_side_effects=True, vmem_limit_bytes=67043328
         ),
-        name="grad_sums",
+        name="grad_update",
     )(experts, counts, cotangent, tokens, gate, up, weight_t)
 
 
@@ -465,22 +524,13 @@
         yield n // 8, (n % 8) * STRIP, row // CHUNK, row % CHUNK
 
 
-def newton_kernel(
-    sums, out,
-    pair, from_core, pair_core, mat, gram, whole, near0, fin0, near1, fin1,
+def newton_steps(
+    swaps, c, y, h, other, out, sums,
+    pair, from_core, pair_core, mat, gram, whole, near0, fin0, gath,
     g1, p1, u, g2, p2, ring0, ring1,
     x_send, x_recv, g_send, g_recv, a_send, a_recv, o_send, o_recv,
 ):
-    c, y = lax.axis_index("core"), lax.axis_index("y")
-    h = lax.rem(y, 2)
-    mate = y + 1 - 2 * h
-    other = {"core": 1 - c}
-    greet(AXES, (other, {"y": mate, "core": 1 - c}))
-    low_rows = sums.at[pl.ds(HALF, THIRD)]
-    down = push(low_rows, pair, x_send.at[0], x_recv.at[0], {"y": mate})
-    onward = push(low_rows, pair_core, x_send.at[2], x_recv.at[2], {"y": mate, "core": 1 - c})
-    swap = push(sums, from_core, x_send.at[1], x_recv.at[1], other)
-    for copy in (swap, down, onward):
+    for copy in swaps:
         copy.wait_recv()
 
     @pl.when(c == 0)
@@ -508,15 +558,13 @@
             ]
 
     four = lead_halves(4)
-    halves = lead_halves(CHUNK)
     orders = (("z", "x"), ("x", "z"))
-    rs0, rs1, ag0, ag1 = [], [], [], []
+    rs0, ag0, ag1 = [], [], []
     for k in range(2):
         first_axis, second_axis = orders[k]
         a = lax.axis_index(first_axis)
         rs0.append(Scatter(first_axis, gram.at[k], *four, near0.at[k], fin0.at[k], g_send.at[k, 0], g_recv.at[k, 0], add_blocks))
-        rs1.append(Scatter(second_axis, gram.at[k, a], *halves, near1.at[k], fin1.at[k], g_send.at[k, 1], g_recv.at[k, 1], add_blocks))
-        ag0.append(Gather(second_axis, whole.at[k, a], *halves, a_send.at[k, 0], a_recv.at[k, 0]))
+        ag0.append(Gather(second_axis, gath.at[k], *four, a_send.at[k, 0], a_recv.at[k, 0]))
         ag1.append(Gather(first_axis, whole.at[k], *four, a_send.at[k, 1], a_recv.at[k, 1]))
     for k in range(2):
         rs0[k].start()
@@ -524,18 +572,19 @@
         rs0[k].middle()
     for k in range(2):
         rs0[k].finish()
-        rs1[k].start()
-    for k in range(2):
-        rs1[k].middle()
-    for k in range(2):
-        rs1[k].finish()
         a, b = (lax.axis_index(axis) for axis in orders[k])
-        whole[k, a, b] = gram[k, a, b]
+        gath[k, b] = gram[k, a]
         ag0[k].start()
     for k in range(2):
         ag0[k].middle()
     for k in range(2):
         ag0[k].finish()
+        a = lax.axis_index(orders[k][0])
+        for b in range(4):
+            total = gath[k, 0, b].astype(f32)
+            for source in range(1, 4):
+                total = total + gath[k, source, b].astype(f32)
+            whole[k, a, b] = total.astype(bf16)
         ag1[k].start()
     for k in range(2):
         ag1[k].middle()
@@ -577,24 +626,22 @@
     def make_p2(cols):
         p2[:, cols] = (ns_second * g2[:, cols].astype(f32) + ns_third * times(g2, g2, cols)).astype(bf16)
 
-    def make_rest(cols):
-        rest = ns_first * (p1[:, cols].astype(f32) + p2[:, cols].astype(f32)) + times(p2, p1, cols)
-        u[:, cols] = rest.astype(bf16)
-
-    for body in (make_p1, make_u, make_g2, make_p2, make_rest):
+    for body in (make_p1, make_u, make_g2, make_p2):
         @pl.loop(0, F // WIDE)
         def one(t, body=body):
             body(pl.ds(pl.multiple_of(t * WIDE, WIDE), WIDE))
 
-    factor = scale * jnp.sqrt(f32(D))
+    factor = jnp.sqrt(f32(D))
     XT = X.astype(f32).T
     low = XT.astype(bf16)
+    first_x = (ns_first * XT + jnp.dot(low, p1[...], preferred_element_type=f32)) * scale
+    low = first_x.astype(bf16)
     i, right, left, far = around("y")
     side = LANES // 2
 
     @pl.when(c == 0)
     def send_first():
-        new = ns_first * ns_first * XT + jnp.dot(low, u[...], preferred_element_type=f32)
+        new = ns_first * low.astype(f32) + jnp.dot(low, p2[...], preferred_element_type=f32)
         ring0[i] = (factor * new).astype(bf16)
         ring = Gather("y", ring0, *lead_halves(LANES), o_send.at[0], o_recv.at[0])
         place = lambda t: out.at[lax.div(t, 2), lax.rem(t, 2)]
@@ -622,9 +669,9 @@
     @pl.when(c == 1)
     def send_second():
         half = pl.ds(pl.multiple_of(h * HALF, HALF), HALF)
-        g2[0:LANES, 0:HALF] = jnp.where(h == 0, XT[:, 0:HALF], XT[:, HALF:]).astype(bf16)
-        new = ns_first * ns_first * g2[0:LANES, 0:HALF].astype(f32) + jnp.dot(
-            low, u[:, half], preferred_element_type=f32
+        kept = jnp.where(h == 0, first_x[:, 0:HALF], first_x[:, HALF:])
+        new = ns_first * kept.astype(bf16).astype(f32) + jnp.dot(
+            low, p2[:, half], preferred_element_type=f32
         )
         ring1[i] = (factor * new).astype(bf16)
         ring = Gather("y", ring1, *lead_halves(LANES), o_send.at[1], o_recv.at[1])
@@ -649,59 +696,20 @@
             copy.wait_send()
         ring.drain()
 
-    for copy in (down, swap, onward):
+    for copy in swaps:
         copy.wait_send()
-    for one in rs0 + rs1 + ag0 + ag1:
+    for one in rs0 + ag0 + ag1:
         one.drain()
-
-
-def newton(sums):
-    vmem = pltpu.VMEM
-    dma = pltpu.SemaphoreType.DMA
-    square = vmem((F, F), bf16)
-    return pl.pallas_call(
-        newton_kernel,
-        out_shape=jax.ShapeDtypeStruct((2, 3, LANES // 2, F), bf16),
-        in_specs=[pl.BlockSpec(memory_space=vmem)],
-        out_specs=pl.BlockSpec(memory_space=vmem),
-        scratch_shapes=[
-            vmem((THIRD, LANES), bf16),
-            vmem((3 * THIRD, LANES), bf16),
-            vmem((THIRD, LANES), bf16),
-            vmem((4, THIRD, LANES), bf16),
-            vmem((2, 4, 4, CHUNK, LANES), bf16),
-            vmem((2, 4, 4, CHUNK, LANES), bf16),
-            vmem((2, 4, CHUNK, LANES), bf16),
-            vmem((2, 2, 4, CHUNK, LANES), bf16),
-            vmem((2, CHUNK, LANES), bf16),
-            vmem((2, 2, CHUNK, LANES), bf16),
-            square, square, square, square, square,
-            vmem((4, LANES, F), bf16),
-            vmem((4, LANES, HALF), bf16),
-            dma((7,)),
-            dma((7,)),
-            dma((2, 2, 6)),
-            dma((2, 2, 6)),
-            dma((2, 2, 4)),
-            dma((2, 2, 4)),
-            dma((2, 4)),
-            dma((2, 4)),
-        ],
-        compiler_params=pltpu.CompilerParams(
-            collective_id=1, has_side_effects=True, vmem_limit_bytes=60 * 1024 * 1024
-        ),
-        name="newton",
-    )(sums)
 
 
 def per_device(
     token_inputs, cotangent, gate_preact, up_preact, down_weight, block_expert, block_count
 ):
-    sums = grad_sums(
+    done = grad_update(
         block_expert, block_count, cotangent, token_inputs, gate_preact, up_preact,
         down_weight.swapaxes(1, 2),
     )
-    return newton(sums).swapaxes(2, 3)
+    return done.swapaxes(2, 3)
 
 
 def solution(mesh):

time: 151 us -> 139 us (0.921)
  Pallas kernels: 149 us -> 137 us
    pallas_call x2 -> x1, Pallas kernels: 149 us -> 137 us  [grad_update(): pl.pallas_call(grad_kernel, out_shape=jax.ShapeDtypeStruct((2, 3, LANES /...]
where the time goes in v3:
time: 139 us
  Pallas kernels  137 us (99%)
  local copies, waits for them, and re-layouts  1.92 us (1%)
    pallas_call x1, Pallas kernels, grad_update(): pl.pallas_call(grad_kernel, out_shape=jax.ShapeDtypeStruct((2, 3, LANES /...  137 us

profile of v3, /device:TPU:1, one launch (start us, length us, event | category | flops | bytes accessed | tf_op | source)
XLA Modules:
  0.0 139.2 jit_solution(17044889582962096379)
XLA Ops:
  0.0 137.2 %grad_update.1 = bf16[2,3,64,768]{3,2,1,0:T(8,128)(2,1)} custom-call(s32[4]{0:T(128)} %experts.1, s32[4]{0:T(128)} %counts.1, bf16[512,2048]{1,0:T(8,128)(2,1)} %cotangent.1, bf16[512,2048]{1,0:T(8,128)(2,1)} %tokens.1, bf16[512,768]{1,0:T(8,128)(2,1)} %gate.1, bf16[512,768]{1,0:T(8,128)(2,1)} %up.1, bf16[2,64,768]{2,1,0:T(8,128)(2,1)} %bitcast.3), custom_call_target="tpu_custom_call" | custom-call | tf_op jit(solution)/shard_map/grad_update/pallas_call | solution.py:459
  137.2 1.9 %copy.9 = bf16[2,3,768,64]{2,3,1,0:T(8,128)(2,1)} copy(bf16[2,3,768,64]{2,3,1,0:T(8,128)(2,1)} %bitcast.2) | data formatting | bytes 1179648

commit v4 on v3

--- a/solution.py
+++ b/solution.py
@@ -17,12 +17,13 @@
 LANES = 128
 AXES = ("z", "x", "y")
 UNITS = (
-    (0, 64, ("x", "y", "z"), False),
-    (64, 64, ("y", "z", "x"), False),
-    (128, 64, ("z", "y", "x"), False),
-    (192, 64, ("y", "x", "z"), False),
-    (256, 64, ("z", "y", "x"), False),
-    (320, 64, ("x", "z", "y"), False),
+    (0, 64, ("z", "x", "y"), False),
+    (64, 64, ("x", "y", "z"), False),
+    (128, 64, ("x", "y", "z"), False),
+    (192, 64, ("z", "y", "x"), False),
+    (256, 64, ("y", "z", "x"), False),
+    (320, 32, ("z", "x", "y"), False),
+    (352, 32, ("z", "x", "y"), False),
     (0, 192, ("y", "x", "z"), True),
 )
 STEPS = (
@@ -30,65 +31,72 @@
     ("pd", 0, ""),
     ("wn", 0, "m"),
     ("wn", 1, "m"),
+    ("pd", 1, ""),
     ("wn", 0, "f"),
     ("wn", 1, "f"),
-    (6, 0, "m"),
     ("wf", 0, "m"),
     ("wf", 1, "m"),
+    (7, 0, "m"),
     ("wf", 0, "f"),
     ("wf", 1, "f"),
-    ("wfull", 0, ""),
     ("back", 0, ""),
     ("prod", 0, ""),
     ("prod", 1, ""),
     ("back", 128, ""),
     ("prod", 2, ""),
     (0, 0, "m"),
-    (6, 0, "f"),
+    (1, 0, "m"),
     ("prod", 3, ""),
-    (1, 0, "m"),
     ("back", 256, ""),
+    (0, 0, "f"),
+    (7, 0, "f"),
     (2, 0, "m"),
-    (0, 0, "f"),
     ("prod", 4, ""),
     (3, 0, "m"),
+    ("prod", 5, ""),
+    ("prod", 6, ""),
+    (1, 0, "f"),
+    (0, 1, "m"),
+    (4, 0, "m"),
+    (3, 0, "f"),
+    (5, 0, "m"),
+    (7, 1, "m"),
+    (1, 1, "m"),
+    (6, 0, "m"),
+    (4, 0, "f"),
+    (2, 0, "f"),
+    (5, 0, "f"),
+    (3, 1, "m"),
+    (0, 1, "f"),
+    (6, 0, "f"),
+    (1, 1, "f"),
+    (4, 1, "m"),
+    (7, 1, "f"),
+    (2, 1, "m"),
+    (5, 1, "m"),
+    (1, 2, "m"),
     (6, 1, "m"),
-    ("prod", 5, ""),
-    (2, 0, "f"),
+    (3, 1, "f"),
+    (0, 2, "m"),
+    (4, 1, "f"),
+    (7, 2, "m"),
+    (5, 1, "f"),
+    (2, 1, "f"),
+    (1, 2, "f"),
     (6, 1, "f"),
-    (1, 0, "f"),
-    (4, 0, "m"),
-    (0, 1, "m"),
-    (5, 0, "m"),
-    (6, 2, "m"),
-    (3, 0, "f"),
-    (1, 1, "m"),
-    (2, 1, "m"),
-    (0, 1, "f"),
-    (2, 1, "f"),
-    (5, 0, "f"),
-    (4, 0, "f"),
-    (3, 1, "m"),
-    (6, 2, "f"),
+    (3, 2, "m"),
+    (0, 2, "f"),
+    (4, 2, "m"),
+    (5, 2, "m"),
+    (7, 2, "f"),
     ("low", 0, ""),
     (2, 2, "m"),
-    (1, 1, "f"),
-    (0, 2, "m"),
-    (5, 1, "m"),
-    (4, 1, "m"),
-    (3, 1, "f"),
+    (6, 2, "m"),
+    (3, 2, "f"),
+    (4, 2, "f"),
+    (5, 2, "f"),
     (2, 2, "f"),
-    (0, 2, "f"),
-    (1, 2, "m"),
-    (5, 1, "f"),
-    (3, 2, "m"),
-    (4, 1, "f"),
-    (1, 2, "f"),
-    (5, 2, "m"),
-    (3, 2, "f"),
-    (4, 2, "m"),
-    (5, 2, "f"),
-    (4, 2, "f"),
+    (6, 2, "f"),
 )
 MESH = pl.DeviceIdType.MESH
 
@@ -170,25 +178,66 @@
 
     def start(self):
         i, right, left, far = around(self.axis)
-        buf = self.buf
-        self.a1 = push(buf.at[i], buf.at[i], self.send.at[0], self.recv.at[0], {self.axis: right})
-        self.b1 = push(buf.at[i], buf.at[i], self.send.at[1], self.recv.at[1], {self.axis: left})
+        first, second = self.first(self.buf.at[i]), self.second(self.buf.at[i])
+        to_right, to_left = {self.axis: right}, {self.axis: left}
+        self.a1 = push(first, first, self.send.at[0], self.recv.at[0], to_right)
+        self.b1 = push(second, second, self.send.at[1], self.recv.at[1], to_left)
+        self.a3 = push(second, second, self.send.at[2], self.recv.at[2], to_right)
+        self.b3 = push(first, first, self.send.at[3], self.recv.at[3], to_left)
+
+    def middle(self):
+        i, right, left, far = around(self.axis)
+        first, second = self.first(self.buf.at[left]), self.second(self.buf.at[right])
+        self.a1.wait_recv()
+        self.a2 = push(first, first, self.send.at[4], self.recv.at[4], {self.axis: right})
+        self.b1.wait_recv()
+        self.b2 = push(second, second, self.send.at[5], self.recv.at[5], {self.axis: left})
+
+    def nearby(self):
+        self.a3.wait_recv()
+        self.b3.wait_recv()
+
+    def finish(self):
+        self.a2.wait_recv()
+        self.b2.wait_recv()
+
+    def drain(self):
+        for copy in (self.a1, self.b1, self.a2, self.b2, self.a3, self.b3):
+            copy.wait_send()
+
+
+class Pieces:
+    def __init__(self, axis, inner, buf, first, second, send, recv):
+        self.axis, self.inner, self.buf, self.first, self.second = axis, inner, buf, first, second
+        self.send, self.recv = send, recv
+        self.rightward, self.leftward = {}, {}
+
+    def piece(self, role):
+        i, right, left, far = around(self.axis)
+        src = self.buf.at[i, around(self.inner)[role]]
+        self.rightward[role] = push(src, src, self.send.at[role], self.recv.at[role], {self.axis: right})
+        self.leftward[role] = push(src, src, self.send.at[4 + role], self.recv.at[4 + role], {self.axis: left})
 
     def middle(self):
         i, right, left, far = around(self.axis)
         buf, first, second = self.buf, self.first, self.second
-        self.a1.wait_recv()
-        self.a2 = push(first(buf.at[left]), first(buf.at[left]), self.send.at[2], self.recv.at[2], {self.axis: right})
-        self.b1.wait_recv()
-        self.b2 = push(second(buf.at[right]), second(buf.at[right]), self.send.at[3], self.recv.at[3], {self.axis: left})
+        for role in range(4):
+            self.rightward[role].wait_recv()
+        self.a2 = push(first(buf.at[left]), first(buf.at[left]), self.send.at[8], self.recv.at[8], {self.axis: right})
+        for role in range(4):
+            self.leftward[role].wait_recv()
+        self.b2 = push(second(buf.at[right]), second(buf.at[right]), self.send.at[9], self.recv.at[9], {self.axis: left})
 
     def finish(self):
         self.a2.wait_recv()
         self.b2.wait_recv()
 
     def drain(self):
-        for copy in (self.a1, self.b1, self.a2, self.b2):
-            copy.wait_send()
+        for role in range(4):
+            self.rightward[role].wait_send()
+            self.leftward[role].wait_send()
+        self.a2.wait_send()
+        self.b2.wait_send()
 
 
 def add_blocks(dst, others):
@@ -280,8 +329,8 @@
         Gather("x", wall.at[1, z], first, second, w_send.at[1], w_recv.at[1]),
     ]
     w_far = [
-        Gather("x", wall.at[0], four_first, four_second, w_send.at[2], w_recv.at[2]),
-        Gather("z", wall.at[1], four_first, four_second, w_send.at[3], w_recv.at[3]),
+        Pieces("x", "z", wall.at[0], four_first, four_second, w_send.at[2], w_recv.at[2]),
+        Pieces("z", "x", wall.at[1], four_first, four_second, w_send.at[3], w_recv.at[3]),
     ]
     ready(0)
     for e in range(2):
@@ -292,6 +341,8 @@
             wall[1, z, x] = block
     for one in w_near:
         one.start()
+    for one in w_far:
+        one.piece(0)
 
     rs = []
     cut = lead_halves(4)
@@ -325,13 +376,13 @@
                     for h in range(2):
                         left_d[2 * e + h, :, there] = kept[h * THIRD:(h + 1) * THIRD]
 
-    def products(picked):
+    def products(picked, begin=0, end=4):
         down = UNITS[picked[0]][3]
         lhs_ref, right = (left_d, mk) if down else (left_g, tk)
         low = UNITS[picked[0]][0]
         size = sum(UNITS[k][1] for k in picked)
 
-        @pl.loop(0, 4)
+        @pl.loop(begin, end)
         def columns(iz):
             cols = pl.ds(pl.multiple_of(iz * 512, 512), 512)
             lhs = lhs_ref[:, low:low + size, :].reshape(4 * size, 2 * ROWS)
@@ -346,15 +397,16 @@
                         index = tuple(where[axis] for axis in order)
                         buffers[k][0][index] = acc[first:first + rows, ix * LANES:(ix + 1) * LANES]
 
-        for k in picked:
-            rs[k][0].start()
-
-    def pack_weights():
+        if end == 4:
+            for k in picked:
+                rs[k][0].start()
+
+    def pack_weights(rows):
         for iz in range(4):
             for ix in range(4):
                 cols = slice((iz * 4 + ix) * LANES, (iz * 4 + ix + 1) * LANES)
-                wfull[0, :, cols] = wall[0, ix, iz]
-                wfull[1, :, cols] = wall[1, iz, ix]
+                wfull[0, rows, cols] = wall[0, ix, iz, rows, :]
+                wfull[1, rows, cols] = wall[1, iz, ix, rows, :]
 
     def make_back(low):
         tile = 32
@@ -401,18 +453,21 @@
         if name == "hid":
             make_hidden()
         elif name == "pd":
-            ready(3)
-            products([k for k in range(len(UNITS)) if UNITS[k][3]])
-        elif name == "wfull":
-            pack_weights()
+            if e == 0:
+                ready(3)
+            products([k for k in range(len(UNITS)) if UNITS[k][3]], 2 * e, 2 * e + 2)
         elif name == "back":
+            pack_weights(slice(e, e + LANES))
             make_back(e)
         elif name == "wn":
             if what == "m":
                 w_near[e].middle()
+                w_near[e].nearby()
+                w_far[e].piece(1)
+                w_far[e].piece(2)
             else:
                 w_near[e].finish()
-                w_far[e].start()
+                w_far[e].piece(3)
         elif name == "wf":
             if what == "m":
                 w_far[e].middle()
@@ -479,8 +534,8 @@
             dma((5,)),
             dma((6,)),
             dma((6,)),
-            dma((4, 4)),
-            dma((4, 4)),
+            dma((4, 10)),
+            dma((4, 10)),
             dma((len(UNITS), 3, 6)),
             dma((len(UNITS), 3, 6)),
             vmem((3 * THIRD, LANES), bf16),
@@ -500,10 +555,10 @@
             dma((8,)),
             dma((2, 2, 6)),
             dma((2, 2, 6)),
-            dma((2, 2, 4)),
-            dma((2, 2, 4)),
-            dma((2, 4)),
-            dma((2, 4)),
+            dma((2, 2, 6)),
+            dma((2, 2, 6)),
+            dma((2, 6)),
+            dma((2, 6)),
         ],
         compiler_params=pltpu.CompilerParams(
             collective_id=0, has_side_effects=True, vmem_limit_bytes=67043328
@@ -578,6 +633,7 @@
     for k in range(2):
         ag0[k].middle()
     for k in range(2):
+        ag0[k].nearby()
         ag0[k].finish()
         a = lax.axis_index(orders[k][0])
         for b in range(4):
@@ -589,6 +645,7 @@
     for k in range(2):
         ag1[k].middle()
     for k in range(2):
+        ag1[k].nearby()
         ag1[k].finish()
 
     trace = jnp.zeros((STRIP, LANES), f32)
@@ -649,6 +706,7 @@
         ring.start()
         over = [give(i, 3)]
         ring.middle()
+        ring.nearby()
         over.append(give(left, 4))
         over.append(give(right, 5))
         ring.finish()
@@ -680,6 +738,7 @@
         ring.start()
         over = [give(i, 3)]
         ring.middle()
+        ring.nearby()
         over.append(give(left, 4))
         over.append(give(right, 5))
         ring.finish()

time: 139 us -> 133 us (0.957)
  Pallas kernels: 137 us -> 131 us
    pallas_call x1, Pallas kernels: 137 us -> 131 us  [grad_update(): pl.pallas_call(grad_kernel, out_shape=jax.ShapeDtypeStruct((2, 3, LANES /...]
where the time goes in v4:
time: 133 us
  Pallas kernels  131 us (98%)
  local copies, waits for them, and re-layouts  1.92 us (1%)
    pallas_call x1, Pallas kernels, grad_update(): pl.pallas_call(grad_kernel, out_shape=jax.ShapeDtypeStruct((2, 3, LANES /...  131 us

profile of v4, /device:TPU:1, one launch (start us, length us, event | category | flops | bytes accessed | tf_op | source)
XLA Modules:
  0.0 133.2 jit_solution(3106461217453708125)
XLA Ops:
  0.0 131.2 %grad_update.1 = bf16[2,3,64,768]{3,2,1,0:T(8,128)(2,1)} custom-call(s32[4]{0:T(128)} %experts.1, s32[4]{0:T(128)} %counts.1, bf16[512,2048]{1,0:T(8,128)(2,1)} %cotangent.1, bf16[512,2048]{1,0:T(8,128)(2,1)} %tokens.1, bf16[512,768]{1,0:T(8,128)(2,1)} %gate.1, bf16[512,768]{1,0:T(8,128)(2,1)} %up.1, bf16[2,64,768]{2,1,0:T(8,128)(2,1)} %bitcast.3), custom_call_target="tpu_custom_call" | custom-call | tf_op jit(solution)/shard_map/grad_update/pallas_call | solution.py:514
  131.2 1.9 %copy.9 = bf16[2,3,768,64]{2,3,1,0:T(8,128)(2,1)} copy(bf16[2,3,768,64]{2,3,1,0:T(8,128)(2,1)} %bitcast.2) | data formatting | bytes 1179648

commit v5 on v4

--- a/solution.py
+++ b/solution.py
@@ -1,5 +1,3 @@
-import functools
-
 import jax
 import jax.numpy as jnp
 from jax import lax
@@ -218,26 +216,28 @@
         self.rightward[role] = push(src, src, self.send.at[role], self.recv.at[role], {self.axis: right})
         self.leftward[role] = push(src, src, self.send.at[4 + role], self.recv.at[4 + role], {self.axis: left})
 
-    def middle(self):
+    def forward(self, role):
         i, right, left, far = around(self.axis)
-        buf, first, second = self.buf, self.first, self.second
-        for role in range(4):
+        place = around(self.inner)[role]
+        first, second = self.first(self.buf.at[left, place]), self.second(self.buf.at[right, place])
+        self.rightward[role].wait_recv()
+        self.rightward[8 + role] = push(
+            first, first, self.send.at[8 + role], self.recv.at[8 + role], {self.axis: right}
+        )
+        self.leftward[role].wait_recv()
+        self.leftward[8 + role] = push(
+            second, second, self.send.at[12 + role], self.recv.at[12 + role], {self.axis: left}
+        )
+
+    def finish(self):
+        for role in range(8, 12):
             self.rightward[role].wait_recv()
-        self.a2 = push(first(buf.at[left]), first(buf.at[left]), self.send.at[8], self.recv.at[8], {self.axis: right})
-        for role in range(4):
             self.leftward[role].wait_recv()
-        self.b2 = push(second(buf.at[right]), second(buf.at[right]), self.send.at[9], self.recv.at[9], {self.axis: left})
-
-    def finish(self):
-        self.a2.wait_recv()
-        self.b2.wait_recv()
 
     def drain(self):
-        for role in range(4):
+        for role in self.rightward:
             self.rightward[role].wait_send()
             self.leftward[role].wait_send()
-        self.a2.wait_send()
-        self.b2.wait_send()
 
 
 def add_blocks(dst, others):
@@ -323,14 +323,13 @@
 
     z, x = lax.axis_index("z"), lax.axis_index("x")
     first, second = lead_halves(HALF)
-    four_first, four_second = lead_halves(4)
     w_near = [
         Gather("z", wall.at[0, x], first, second, w_send.at[0], w_recv.at[0]),
         Gather("x", wall.at[1, z], first, second, w_send.at[1], w_recv.at[1]),
     ]
     w_far = [
-        Pieces("x", "z", wall.at[0], four_first, four_second, w_send.at[2], w_recv.at[2]),
-        Pieces("z", "x", wall.at[1], four_first, four_second, w_send.at[3], w_recv.at[3]),
+        Pieces("x", "z", wall.at[0], first, second, w_send.at[2], w_recv.at[2]),
+        Pieces("z", "x", wall.at[1], first, second, w_send.at[3], w_recv.at[3]),
     ]
     ready(0)
     for e in range(2):
@@ -468,9 +467,11 @@
             else:
                 w_near[e].finish()
                 w_far[e].piece(3)
+                w_far[e].forward(0)
         elif name == "wf":
             if what == "m":
-                w_far[e].middle()
+                for role in (1, 2, 3):
+                    w_far[e].forward(role)
             else:
                 w_far[e].finish()
         elif name == "prod":
@@ -534,8 +535,8 @@
             dma((5,)),
             dma((6,)),
             dma((6,)),
-            dma((4, 10)),
-            dma((4, 10)),
+            dma((4, 16)),
+            dma((4, 16)),
             dma((len(UNITS), 3, 6)),
             dma((len(UNITS), 3, 6)),
             vmem((3 * THIRD, LANES), bf16),

time: 133 us -> 132 us (level)
    pallas_call x1, Pallas kernels: 131 us -> 130 us  [grad_update(): pl.pallas_call(grad_kernel, out_shape=jax.ShapeDtypeStruct((2, 3, LANES /...]
where the time goes in v5:
time: 132 us
  Pallas kernels  130 us (98%)
  local copies, waits for them, and re-layouts  1.92 us (1%)
    pallas_call x1, Pallas kernels, grad_update(): pl.pallas_call(grad_kernel, out_shape=jax.ShapeDtypeStruct((2, 3, LANES /...  130 us

profile of v5, /device:TPU:1, one launch (start us, length us, event | category | flops | bytes accessed | tf_op | source)
XLA Modules:
  0.0 131.7 jit_solution(11732802008842623887)
XLA Ops:
  0.0 129.8 %grad_update.1 = bf16[2,3,64,768]{3,2,1,0:T(8,128)(2,1)} custom-call(s32[4]{0:T(128)} %experts.1, s32[4]{0:T(128)} %counts.1, bf16[512,2048]{1,0:T(8,128)(2,1)} %cotangent.1, bf16[512,2048]{1,0:T(8,128)(2,1)} %tokens.1, bf16[512,768]{1,0:T(8,128)(2,1)} %gate.1, bf16[512,768]{1,0:T(8,128)(2,1)} %up.1, bf16[2,64,768]{2,1,0:T(8,128)(2,1)} %bitcast.3), custom_call_target="tpu_custom_call" | custom-call | tf_op jit(solution)/shard_map/grad_update/pallas_call | solution.py:515
  129.8 1.9 %copy.9 = bf16[2,3,768,64]{2,3,1,0:T(8,128)(2,1)} copy(bf16[2,3,768,64]{2,3,1,0:T(8,128)(2,1)} %bitcast.2) | data formatting | bytes 1179648
